TPU v7x, 128 devices: a whole 4x4x4 slice. The times are simulated.
128 devices in a mesh: rad: 8 (over y, core), ang: 16 (over x, z).
Axes of the slice: x: 4, y: 4, z: 4, core: 2. Of those that a mesh axis runs over, the one named last changes fastest.
Arguments:
- source_coeffs: bfloat16 [512, 512, 2, 128], P('ang', 'rad'), may hold values from -6 to 6
- inverses: bfloat16 [512, 128, 128], P('rad')
- velocity: bfloat16 [2, 768, 128, 1536], P(None, 'ang', 'rad'), may hold values from -6 to 6
- order_slots: int32 [512], replicated, may hold values from 0 to 511, as said below
Outputs:
- advected: bfloat16 [512, 2, 128, 512], P('ang', None, 'rad')
Inputs may be any that keep to these rules, and one draw needn't show every extreme that they name: `order_slots`: the slots form 512 // 32 consecutive blocks of 32; in each block the first 16 slots hold distinct orders below 256, and slot 16 + i of a block holds 511 minus the order in slot i of that block; every order appears exactly once.
All inputs are finite; a program needn't handle non-finite values.
Results may differ from a plain program's by a relative error of at most 0.012.
Values may be sent and summed in bfloat16 or wider, within the bound.
No kernel may reach another device: no remote copies, remote signals or barrier semaphores. Data moves between devices by JAX's collectives and lax.ppermute only.
A program may use at most 256 MiB of HBM per device.

v0:
```python
import math

import jax
import jax.numpy as jnp
from jax import lax
from jax.sharding import PartitionSpec as P

inner_radius = 0.35
rescale_bound = 1e20
rescale_log = 46.051701859880914
start_log = -1.2051210046670229


def legendre_rows(orders, degree_count, lat_count):
    colatitude = (jnp.arange(lat_count, dtype=jnp.float32) + 0.5) * (math.pi / lat_count)
    cosines = jnp.cos(colatitude)[None, :]
    sines = jnp.sin(colatitude)[None, :]
    order_value = orders.astype(jnp.float32)[:, None]
    orders_col = orders[:, None]
    log_start = (
        start_log
        + 0.5 * (lax.lgamma(order_value + 1.5) - lax.lgamma(order_value + 1.0))
        + order_value * jnp.log(sines)
    )
    zero_field = jnp.zeros((orders.shape[0], lat_count), jnp.float32)

    def advance(state_carry, degree):
        prev_one, prev_two, log_scale = state_carry
        degree_value = degree.astype(jnp.float32)
        denominator = jnp.maximum(degree_value * degree_value - order_value * order_value, 1.0)
        recur_a = jnp.sqrt(jnp.maximum(4.0 * degree_value * degree_value - 1.0, 1.0) / denominator)
        lower_sq = (degree_value - 1.0) * (degree_value - 1.0)
        recur_b = jnp.sqrt(
            jnp.maximum(lower_sq - order_value * order_value, 0.0)
            / jnp.maximum(4.0 * lower_sq - 1.0, 1.0)
        )
        grown_value = recur_a * (cosines * prev_one - recur_b * prev_two)
        before = degree < orders_col
        starting = degree == orders_col
        current = jnp.where(before, 0.0, jnp.where(starting, 1.0, grown_value))
        previous = jnp.where(before | starting, 0.0, prev_one)
        too_large = jnp.abs(current) > rescale_bound
        factor = jnp.where(too_large, 1.0 / rescale_bound, 1.0)
        log_scale = log_scale + jnp.where(too_large, rescale_log, 0.0)
        current = current * factor
        previous = previous * factor
        value_scaled = current * jnp.exp(log_scale)
        return ((current, previous, log_scale), value_scaled.astype(jnp.bfloat16))

    _, legendre = lax.scan(
        advance, (zero_field, zero_field, log_start), jnp.arange(degree_count, dtype=jnp.int32)
    )
    return legendre


def radial_tables(mode_count, radius_count):
    angles = (jnp.arange(radius_count, dtype=jnp.float32) + 0.5) * (math.pi / radius_count)
    mode_values = jnp.arange(mode_count, dtype=jnp.float32)[:, None]
    values = jnp.cos(mode_values * angles[None, :])
    slopes = (
        mode_values
        * jnp.sin(mode_values * angles[None, :])
        / jnp.sin(angles)[None, :]
        * (2.0 / (1.0 - inner_radius))
    )
    return jnp.stack([values, slopes])


def fourier_tables(orders, lon_count):
    phase_index = orders[:, None] * jnp.arange(lon_count, dtype=jnp.int32)[None, :] % lon_count
    phase_angle = phase_index.astype(jnp.float32) * (2.0 * math.pi / lon_count)
    weight = jnp.where(orders == 0, 1.0, 2.0).astype(jnp.float32)[:, None]
    cosine = jnp.cos(phase_angle)
    sine = jnp.sin(phase_angle)
    synth_table = jnp.stack([weight * cosine, -weight * sine], 1).astype(jnp.bfloat16)
    analyse_table = (jnp.stack([cosine, -sine], 1) * (2.0 * math.pi / lon_count)).astype(
        jnp.bfloat16
    )
    return (synth_table, analyse_table)


def azimuthal(lat_values, orders):
    order_value = orders.astype(jnp.float32)[:, None, None]
    real_part = lat_values[:, 0].astype(jnp.float32)
    imag_part = lat_values[:, 1].astype(jnp.float32)
    return jnp.stack([-order_value * imag_part, order_value * real_part], 1).astype(jnp.bfloat16)


def local(source_coeffs, inverses, velocity, order_slots):
    slots_local, degrees_local, _, mode_count = source_coeffs.shape
    lat_local = velocity.shape[1]
    radii_local = velocity.shape[2]
    lon_count = velocity.shape[3]
    rad_count = lax.axis_size("rad")
    ang_count = lax.axis_size("ang")
    degree_count = degrees_local * rad_count
    lat_count = lat_local * ang_count
    radius_count = radii_local * rad_count
    rad_index = lax.axis_index("rad")
    ang_index = lax.axis_index("ang")
    my_orders = lax.dynamic_slice_in_dim(order_slots, ang_index * slots_local, slots_local, 0)
    degrees = rad_index * degrees_local + jnp.arange(degrees_local, dtype=jnp.int32)
    degree_mask = (degrees[None, :] >= my_orders[:, None]).astype(jnp.float32)
    solved = (
        jnp.einsum("lkj,slcj->slck", inverses, source_coeffs, preferred_element_type=jnp.float32)
        * degree_mask[:, :, None, None]
    )
    tables = radial_tables(mode_count, radius_count)
    radial = jnp.einsum("slck,fki->sfcli", solved, tables, precision=lax.Precision.HIGHEST).astype(
        jnp.bfloat16
    )
    radial = lax.all_to_all(radial, "rad", split_axis=4, concat_axis=3, tiled=True)
    legendre = legendre_rows(my_orders, degree_count, lat_count)
    lat_spec = jnp.einsum(
        "sfcli,lsj->sfcij", radial, legendre, preferred_element_type=jnp.float32
    ).astype(jnp.bfloat16)
    sending = jnp.concatenate([lat_spec, azimuthal(lat_spec[:, 0], my_orders)[:, None]], 1)
    fields = lax.all_to_all(sending, "ang", split_axis=4, concat_axis=0, tiled=True)
    synth_table, analyse_table = fourier_tables(order_slots, lon_count)
    physical = jnp.einsum(
        "sfcij,scn->fjin", fields, synth_table, preferred_element_type=jnp.float32
    )
    lat_rows = ang_index * lat_local + jnp.arange(lat_local, dtype=jnp.int32)
    colatitude = (lat_rows.astype(jnp.float32) + 0.5) * (math.pi / lat_count)
    sines = jnp.sin(colatitude)
    quad_weight = math.pi / lat_count * sines
    radius_rows = rad_index * radii_local + jnp.arange(radii_local, dtype=jnp.int32)
    angles = (radius_rows.astype(jnp.float32) + 0.5) * (math.pi / radius_count)
    radius_col = (inner_radius + (1.0 - inner_radius) * (jnp.cos(angles) + 1.0) * 0.5)[
        None, :, None
    ]
    flux_term = velocity[0].astype(jnp.float32) * (
        physical[1] + 3.0 * physical[0] / radius_col
    ) + velocity[1].astype(jnp.float32) * physical[2] / (radius_col * sines[:, None, None])
    flux_term = flux_term.astype(jnp.bfloat16)
    fourier = jnp.einsum(
        "jin,scn->scij", flux_term, analyse_table, preferred_element_type=jnp.float32
    )
    fourier = (fourier * quad_weight[None, None, None, :]).astype(jnp.bfloat16)
    fourier = lax.all_to_all(fourier, "ang", split_axis=0, concat_axis=3, tiled=True)
    advected = jnp.einsum(
        "scij,lsj->scil", fourier, legendre, preferred_element_type=jnp.float32
    ).astype(jnp.bfloat16)
    return advected


def solution(mesh):
    in_specs = (P("ang", "rad", None, None), P("rad", None, None), P(None, "ang", "rad", None), P())
    out_specs = P("ang", None, "rad", None)
    return jax.shard_map(local, mesh=mesh, in_specs=in_specs, out_specs=out_specs, check_vma=False)
```

profile of v0, /device:TPU:0, one launch (start us, length us, event | category | flops | bytes accessed | tf_op | source)
XLA Modules:
  0.0 1998.1 jit_solution(2382999333745280602)
XLA Ops:
  0.1 0.9 convert_negate_fusion
  1.6 2.8 bitcast_multiply_fusion
  4.4 4.3 convert_bitcast_fusion
  8.7 7.9 copy.45
  16.6 7.6 reshape.597
  24.1 5.1 all-to-all-start
  29.5 1594.9 %while.20 = (s32[]{:T(128)}, f32[32,768]{1,0:T(8,128)S(1)}, f32[32,768]{1,0:T(8,128)S(1)}, f32[32,768]{1,0:T(8,128)S(1)}, bf16[512,32,768]{2,1,0:T(8,128)(2,1)},...) while((s32[]{:T(128)}, f32[32,768]{1,0:T(8,128)S(1)}, ...), condition=%wide.region_1.2_spmd.clone, body=%wide.region_0.1_spmd.clone.sunk | while | flops 714542 | bytes 1043496 | solution.py:50
  1424.3 0.8 fusion.91
  1624.4 7.5 reshape.598
  1631.9 7.0 copy.46
  1639.0 4.1 copy.47
  1643.1 5.4 all_to_all.42
  1648.5 28.2 %fusion.39 = bf16[32,2,2,16,768]{4,3,2,1,0:T(8,128)(2,1)S(1)} fusion(bf16[32,2,2,512,16]{3,4,2,1,0:T(8,128)(2,1)S(1)} %all_to_all.42, bf16[512,32,768,1,1]{2,1,0,4,3:T(8,128)(2,1)} %bitcast.182), kind=kOutput, calls=%fused_computation.60 | convolution fusion | flops 1612185600 | bytes 30408704 | tf_op jit(solution)/shard_map/sfcli,lsj->sfcij/dot_general | solution.py:114
  1677.2 2.5 maximum_maximum_fusion
  1679.6 31.9 %copy.51 = bf16[32,3,2,16,768]{0,3,2,1,4:T(8,128)(2,1)} copy(bf16[32,3,2,16,768]{4,3,2,1,0:T(8,128)(2,1)} %maximum_maximum_fusion) | data formatting | bytes 9437184 | tf_op jit(solution)/shard_map/concatenate | solution.py:117
  1711.5 22.2 %reshape.599 = bf16[16,2,73728]{2,1,0:T(2,128)(2,1)} reshape(bf16[768,3,2,16,32]{4,3,2,1,0:T(8,128)(2,1)} %bitcast.174) | data formatting | bytes 9437184
  1733.8 8.1 all-to-all-start.1
  1743.2 4.9 fusion.83
  1748.1 15.8 fusion.34
  1763.9 40.7 %all-to-all-done.1 = bf16[16,2,73728]{2,1,0:T(2,128)(2,1)} async-done(((bf16[16,2,73728]{2,1,0:T(2,128)(2,1)}), bf16[16,2,73728]{2,1,0:T(2,128)(2,1)}, u32[]{:S(2)}, u32[]{:S(2)}) %all-to-all-start.1) | async-done | bytes 4718624 | tf_op jit(solution)/shard_map/all_to_all | solution.py:118
  1804.6 16.9 reshape.600
  1821.5 20.8 %copy.111 = bf16[32,3,2,16,16,48]{0,4,5,3,2,1:T(8,128)(2,1)} copy(bf16[32,3,2,16,16,48]{0,3,2,1,5,4:T(8,128)(2,1)} %bitcast.175) | data formatting | bytes 9437184 | tf_op jit(solution)/shard_map/all_to_all | solution.py:118
  1842.3 25.2 %all_to_all.46 = bf16[512,3,2,16,48]{0,4,3,2,1:T(8,128)(2,1)} reshape(bf16[16,32,3,2,16,48]{1,0,5,4,3,2:T(8,128)(2,1)} %bitcast.176) | data formatting | bytes 9437184 | tf_op jit(solution)/shard_map/all_to_all | solution.py:118
  1867.5 13.4 convolution_bitcast_fusion
  1881.0 13.6 fusion.55
  1894.6 6.6 copy.55
  1901.2 9.4 reshape.601
  1910.6 37.8 %all_to_all.54 = bf16[16,2,24576]{2,1,0:T(2,128)(2,1)} all-to-all(bf16[16,2,24576]{2,1,0:T(2,128)(2,1)S(1)} %reshape.601), channel_id=1, replica_groups=mesh['rad'=8,'ang'=16] {'ang'}, dimensions={0} | all-to-all | bytes 3145728 | tf_op jit(solution)/shard_map/all_to_all | solution.py:140
  1948.4 7.3 reshape.602
  1955.7 9.0 copy.57
  1964.7 7.0 all_to_all.50
  1971.7 26.2 %fusion.60 = bf16[32,2,16,512]{3,2,1,0:T(8,128)(2,1)} fusion(bf16[32,2,16,768]{3,2,1,0:T(8,128)(2,1)} %all_to_all.50, bf16[512,32,768,1]{2,1,0,3:T(8,128)(2,1)} %bitcast.183), kind=kOutput, calls=%fused_computation.72 | convolution fusion | flops 805830656 | bytes 27787264 | tf_op jit(solution)/shard_map/scij,lsj->scil/dot_general | solution.py:141
  (3624 shorter events, 1222.3 us)
Async XLA Ops:
  0.0 1.6 copy-start
  24.1 1600.3 %all-to-all-start = ((bf16[8,2,65536]{2,1,0:T(2,128)(2,1)}), bf16[8,2,65536]{2,1,0:T(2,128)(2,1)}, u32[]{:S(2)}, u32[]{:S(2)}) async-start(bf16[8,2,65536]{2,1,0:T(2,128)(2,1)} %reshape.597), calls=%async_computation | async-start | bytes 4194304 | tf_op jit(solution)/shard_map/all_to_all | solution.py:112
  1733.8 8.8 copy-start.6
  1733.8 70.9 %all-to-all-start.1 = ((bf16[16,2,73728]{2,1,0:T(2,128)(2,1)}), bf16[16,2,73728]{2,1,0:T(2,128)(2,1)}, u32[]{:S(2)}, u32[]{:S(2)}) async-start(bf16[16,2,73728]{2,1,0:T(2,128)(2,1)} %reshape.599), calls=%async_computation.1 | async-start | bytes 9437184 | tf_op jit(solution)/shard_map/all_to_all | solution.py:118
  1741.9 6.3 copy-start.8
  1867.5 13.5 copy-start.2
  1867.5 13.5 copy-start.3
  1867.5 13.5 copy-start.4
  1867.5 13.5 copy-start.5
  1867.5 13.5 copy-start.7
  1867.5 13.5 copy-start.9
  1867.5 13.5 copy-start.10
  1971.7 26.2 %copy-start.1 = (bf16[64,128,128]{2,1,0:T(8,128)(2,1)S(1)}, bf16[64,128,128]{2,1,0:T(8,128)(2,1)}, u32[]{:S(2)}) copy-start(bf16[64,128,128]{2,1,0:T(8,128)(2,1)} %param.7) | copy-start | bytes 6291460
where the time goes:
time: 2020 us; the launch traced here: 2000 us
  other arithmetic  900 us (45%)
  local copies, waits for them, and re-layouts  543 us (27%)
  loops' own time  375 us (19%)
  matrix products  88.5 us (4%)
  waiting for transfers between devices  40.7 us (2%)
  blocking collectives  37.8 us (2%)
    dynamic_update_slice x512, other arithmetic, legendre_rows(): lax.scan(advance, (zero_field, zero_field, log_start), jnp.arange(degree_...  397 us
    another operation x1, loops' own time, legendre_rows(): lax.scan(advance, (zero_field, zero_field, log_start), jnp.arange(degree_...  375 us
    or x512, other arithmetic, advance(): previous = jnp.where(before | starting, 0.0, prev_one)  356 us
    dynamic_slice x512, local copies, waits for them, and re-layouts, legendre_rows(): lax.scan(advance, (zero_field, zero_field, log_start), jnp.arange(degree_...  338 us
    unnamed x28, local copies, waits for them, and re-layouts  71.2 us
    cos x512, other arithmetic, legendre_rows(): cosines = jnp.cos(colatitude)[None, :]  63.9 us
    mul x512, other arithmetic, advance(): previous = previous * factor  53.4 us
    all_to_all x2, local copies, waits for them, and re-layouts, local(): lax.all_to_all(sending, 'ang', split_axis=4, concat_axis=0, tiled=True)  46 us
  transfers between devices with their start and end apart: 2, of which 1 were waited for; matrix products, arithmetic and copies ran while one was open for 62% of the time, Pallas kernels for 0%

commit v1 on v0

v1 whole, which is shorter than its diff:
```python
import math

import jax
import jax.numpy as jnp
import numpy as np
from jax import lax
from jax.experimental import pallas as pl
from jax.experimental.pallas import tpu as pltpu
from jax.sharding import PartitionSpec as P

f32 = jnp.float32
bf16 = jnp.bfloat16
inner_radius = 0.35
grow_bound = 1e10
grow_log = 23.025850929940457
start_log = -1.2051210046670229
vmem_bytes = 60 * 1024 * 1024

LMAX, NLAT, NLON, NR, K = 512, 768, 1536, 128, 128
HALF = NLAT // 2
NH = NLON // 2
NT = (((1,), (1,)), ((), ()))
TN = (((0,), (0,)), ((), ()))


def radial_matrix():
    u = (np.arange(NR) + 0.5) * (math.pi / NR)
    k = np.arange(K)[:, None]
    r = inner_radius + (1.0 - inner_radius) * (np.cos(u) + 1.0) * 0.5
    value = np.cos(k * u[None])
    slope = k * np.sin(k * u[None]) / np.sin(u)[None] * (2.0 / (1.0 - inner_radius))
    both = np.stack([value / r, slope + 3.0 * value / r], 0)
    both = both.reshape(2, K, 8, 16).transpose(1, 2, 0, 3).reshape(K, 256)
    out = np.zeros((2, K, 2, 256))
    out[0, :, 0] = both
    out[1, :, 1] = both
    return jnp.asarray(out.reshape(256, 512), f32).astype(bf16)


def params(sem=("arbitrary",)):
    return pltpu.CompilerParams(dimension_semantics=sem, vmem_limit_bytes=vmem_bytes)


def swap_chunks(x0, x1, x2, x3):
    lane = lax.broadcasted_iota(jnp.int32, x0.shape, 1)
    low = lane < 64
    even = (lane // 32) % 2 == 0
    a0 = jnp.where(low, x0, pltpu.roll(x2, 64, 1))
    a2 = jnp.where(low, pltpu.roll(x0, 64, 1), x2)
    a1 = jnp.where(low, x1, pltpu.roll(x3, 64, 1))
    a3 = jnp.where(low, pltpu.roll(x1, 64, 1), x3)
    y0 = jnp.where(even, a0, pltpu.roll(a1, 32, 1))
    y1 = jnp.where(even, pltpu.roll(a0, 96, 1), a1)
    y2 = jnp.where(even, a2, pltpu.roll(a3, 32, 1))
    y3 = jnp.where(even, pltpu.roll(a2, 96, 1), a3)
    return (y0, y1, y2, y3)


def solve_kernel(base_ref, src_ref, inv_ref, order_ref, out_ref, wide, acc):
    step = pl.program_id(0)
    steps = pl.num_programs(0)
    block = inv_ref.shape[0]

    @pl.when(step == 0)
    def _():
        def widen(s, _):
            wide[pl.ds(pl.multiple_of(s * 128, 128), 128), :] = src_ref[s].astype(f32)
            return 0

        lax.fori_loop(0, 32, widen, 0, unroll=4)

    order = order_ref[...]

    def degree(i, _):
        row = step * block + i
        x0 = wide[pl.ds(2 * row, 32, stride=128), :]
        x1 = wide[pl.ds(2 * row + 1, 32, stride=128), :]
        x = jnp.concatenate([x0, x1], 0).astype(bf16)
        y = lax.dot_general(x, inv_ref[i], NT, preferred_element_type=f32)
        y = jnp.where(order <= base_ref[0] + row, y, 0.0)
        acc[pl.ds(row, 64, stride=64), :] = y
        return 0

    lax.fori_loop(0, block, degree, 0, unroll=8)

    @pl.when(step == steps - 1)
    def _():
        for r in range(8):
            for lu in range(2):
                for q in range(2):
                    for c in range(2):
                        plane = c * 32 + lu * 16 + 2 * r + q
                        row = (lu * 4 + q * 2 + c) * 64
                        out_ref[r, row : row + 64, :] = acc[plane * 64 : plane * 64 + 64, :].astype(bf16)


def solve(source, inverses, orders, rad_index):
    src = source.reshape(32, 128, 128)
    order = jnp.broadcast_to(jnp.tile(orders, 2)[:, None], (64, 128))
    return pl.pallas_call(
        solve_kernel,
        grid_spec=pltpu.PrefetchScalarGridSpec(
            num_scalar_prefetch=1,
            grid=(4,),
            in_specs=[
                pl.BlockSpec((32, 128, 128), lambda g, b: (0, 0, 0)),
                pl.BlockSpec((16, 128, 128), lambda g, b: (g, 0, 0)),
                pl.BlockSpec((64, 128), lambda g, b: (0, 0)),
            ],
            out_specs=pl.BlockSpec((8, 512, 128), lambda g, b: (0, 0, 0)),
            scratch_shapes=[pltpu.VMEM((4096, 128), f32), pltpu.VMEM((4096, 128), f32)],
        ),
        out_shape=jax.ShapeDtypeStruct((8, 512, 128), bf16),
        compiler_params=params(),
        cost_estimate=pl.CostEstimate(flops=134217728, bytes_accessed=4194304, transcendentals=0),
        name="solve",
    )(jnp.reshape(rad_index * 64, (1,)), src, inverses, order)


def legendre_kernel(c1_ref, c2_ref, m_ref, x_ref, log_ref, low_ref, up_ref, p1, p2, lg, bp, tile):
    step = pl.program_id(0)

    @pl.when(step == 0)
    def _():
        p1[...] = jnp.zeros(p1.shape, f32)
        p2[...] = jnp.zeros(p2.shape, f32)
        bp[...] = jnp.zeros(bp.shape, f32)
        lg[...] = log_ref[...]

    def run(half, out_ref):
        rows = slice(half * 16, half * 16 + 16)
        m = m_ref[rows, :]
        m2 = m * m
        lanes = [slice(128 * t, 128 * t + 128) for t in range(3)]

        def sub(b, state):
            cur, prev, logs, below = state
            scale = [jnp.exp(v) for v in logs]
            for i in range(8):
                local = b * 8 + i
                l = step * 32 + local
                lf = l.astype(f32)
                d = jnp.maximum(lf * lf - m2, 1.0)
                r = lax.rsqrt(d)
                r = r * (1.5 - 0.5 * d * r * r)
                a = c1_ref[l] * r
                ab = a * below
                below = d * r * c2_ref[l]
                seed = jnp.where(m == lf, 1.0, 0.0)
                for t in range(3):
                    new = (a * x_ref[:, lanes[t]]) * cur[t] - ab * prev[t] + seed
                    prev[t] = cur[t]
                    cur[t] = new
                    tile[t, pl.ds(local, 16, stride=32), :] = new * scale[t]
            for t in range(3):
                big = jnp.abs(cur[t]) > grow_bound
                factor = jnp.where(big, 1.0 / grow_bound, 1.0)
                cur[t] = cur[t] * factor
                prev[t] = prev[t] * factor
                logs[t] = logs[t] + jnp.where(big, grow_log, 0.0)
            return (cur, prev, logs, below)

        state = (
            [p1[rows, v] for v in lanes],
            [p2[rows, v] for v in lanes],
            [lg[rows, v] for v in lanes],
            bp[rows, :],
        )
        cur, prev, logs, below = lax.fori_loop(0, 4, sub, state)
        for t in range(3):
            p1[rows, lanes[t]] = cur[t]
            p2[rows, lanes[t]] = prev[t]
            lg[rows, lanes[t]] = logs[t]
        bp[rows, :] = below
        for s in range(16):
            for t in range(3):
                out_ref[s, :, lanes[t]] = tile[t, s * 32 : s * 32 + 32, :].astype(bf16)

    run(0, low_ref)

    @pl.when(step >= 8)
    def _():
        run(1, up_ref)


def legendre_tables(orders):
    l = np.arange(LMAX, dtype=np.float64)
    root = np.sqrt(np.maximum(4.0 * l * l - 1.0, 1.0))
    t = (np.arange(HALF) + 0.5) * (math.pi / NLAT)
    gammas = [0.5 * (math.lgamma(m + 1.5) - math.lgamma(m + 1.0)) + start_log for m in range(LMAX)]
    x = jnp.asarray(np.broadcast_to(np.cos(t), (16, HALF)), f32)
    mf = orders.astype(f32)
    logs = jnp.take(jnp.asarray(gammas, f32), orders)[:, None] + mf[:, None] * jnp.asarray(np.log(np.sin(t)), f32)[None]
    return pl.pallas_call(
        legendre_kernel,
        grid_spec=pltpu.PrefetchScalarGridSpec(
            num_scalar_prefetch=2,
            grid=(16,),
            in_specs=[
                pl.BlockSpec((32, 128), lambda g, *_: (0, 0)),
                pl.BlockSpec((16, HALF), lambda g, *_: (0, 0)),
                pl.BlockSpec((32, HALF), lambda g, *_: (0, 0)),
            ],
            out_specs=[
                pl.BlockSpec((16, 32, HALF), lambda g, *_: (0, g, 0)),
                pl.BlockSpec((16, 32, HALF), lambda g, *_: (0, jnp.maximum(g - 8, 0), 0)),
            ],
            scratch_shapes=[
                pltpu.VMEM((32, HALF), f32),
                pltpu.VMEM((32, HALF), f32),
                pltpu.VMEM((32, HALF), f32),
                pltpu.VMEM((32, 128), f32),
                pltpu.VMEM((3, 512, 128), f32),
            ],
        ),
        out_shape=[
            jax.ShapeDtypeStruct((16, LMAX, HALF), bf16),
            jax.ShapeDtypeStruct((16, LMAX // 2, HALF), bf16),
        ],
        compiler_params=params(),
        cost_estimate=pl.CostEstimate(flops=60000000, bytes_accessed=12582912, transcendentals=100000),
        name="legendre",
    )(
        jnp.asarray(root, f32),
        jnp.asarray(1.0 / root, f32),
        jnp.broadcast_to(mf[:, None], (32, 128)),
        x,
        logs,
    )


def phase_rows(orders):
    m = jnp.repeat(orders, 2)[:, None]
    c = jnp.tile(jnp.asarray([0, NLON // 4], jnp.int32), orders.shape[0])[:, None]
    near = (m * jnp.arange(128, dtype=jnp.int32)[None] + c) % NLON
    far = (m * (128 * jnp.arange(8, dtype=jnp.int32))[None]) % NLON
    near = near.astype(f32) * (2.0 * math.pi / NLON)
    far = far.astype(f32) * (2.0 * math.pi / NLON)
    return (jnp.cos(near), jnp.sin(near), jnp.cos(far), jnp.sin(far))


def table_kernel(nc, ns, fc, fs, w, mw, anc, ans, afc, afs, t_ref, d_ref, a_ref):
    scale = (2.0 * math.pi / NLON) * (math.pi / NLAT)
    for b in range(6):
        lanes = slice(128 * b, 128 * b + 128)
        cosine = fc[:, b : b + 1] * nc[...] - fs[:, b : b + 1] * ns[...]
        sine = fs[:, b : b + 1] * nc[...] + fc[:, b : b + 1] * ns[...]
        t_ref[:, lanes] = (w[...] * cosine).astype(bf16)
        d_ref[:, lanes] = (mw[...] * sine).astype(bf16)
        a_ref[:, lanes] = (scale * (afc[:, b : b + 1] * anc[...] - afs[:, b : b + 1] * ans[...])).astype(bf16)


def fourier_tables(synth_orders, analyse_orders):
    synth = phase_rows(synth_orders)
    analyse = phase_rows(analyse_orders)
    m = jnp.repeat(synth_orders, 2).astype(f32)
    w = jnp.where(m == 0.0, 1.0, 2.0)
    w2 = jnp.broadcast_to(w[:, None], (1024, 128))
    mw2 = jnp.broadcast_to((-m * w)[:, None], (1024, 128))
    near = pl.BlockSpec((256, 128), lambda g: (g, 0))
    far = pl.BlockSpec((256, 8), lambda g: (g, 0))
    out = pl.BlockSpec((256, NH), lambda g: (g, 0))
    return pl.pallas_call(
        table_kernel,
        grid=(4,),
        in_specs=[near, near, far, far, near, near, near, near, far, far],
        out_specs=[out, out, out],
        out_shape=[jax.ShapeDtypeStruct((1024, NH), bf16)] * 3,
        compiler_params=params(),
        cost_estimate=pl.CostEstimate(flops=8000000, bytes_accessed=8000000, transcendentals=0),
        name="tables",
    )(*synth, w2, mw2, *analyse)


def synth_kernel(ints_ref, recv_ref, low_ref, up_ref, mat_ref, out_ref, ns, scr):
    mat = mat_ref[...]
    for lu in range(2):
        for q in range(2):
            first = 4 * lu
            count = 64 * (8 - first)
            h = ints_ref[1 + q]
            h = h if lu == 0 else 1 - h
            planes = []
            for c in range(2):
                row = (lu * 4 + q * 2 + c) * 64
                planes.append(recv_ref[first:8, row : row + 64, :].reshape(count, 128))
            coeffs = jnp.concatenate(planes, 1)
            rad = jnp.dot(coeffs, mat, preferred_element_type=f32)
            degree = lax.broadcasted_iota(jnp.int32, rad.shape, 0)
            sign = (1 - 2 * ((degree + h) % 2)).astype(f32)
            both = jnp.concatenate([rad.astype(bf16), (rad * sign).astype(bf16)], 1)
            table = low_ref[q] if lu == 0 else up_ref[q]
            wave = lax.dot_general(table, both, TN, preferred_element_type=f32)
            for tile in range(8):
                ns[tile] = wave[:, 128 * tile : 128 * tile + 128]
            for half in range(2):
                for c in range(2):
                    for rh in range(2):
                        tile = half * 4 + c * 2 + rh
                        parts = swap_chunks(*[ns[tile, pl.ds(j, 96, stride=4), :] for j in range(4)])
                        for rl in range(4):
                            base = (((rh * 4 + rl) * 2 + half) * 96) * 8 + q * 2 + c
                            scr[pl.ds(base + h * 4, 96, stride=8), :] = parts[rl]

    def emit(i, _):
        r = i // 16
        a = i % 16
        half = a // 8
        north = jnp.where(half == 0, a, 15 - a)
        start = pl.multiple_of(((r * 2 + half) * 96 + north * 12) * 8, 32)
        out_ref[i] = scr[pl.ds(start, 96), :].astype(bf16)
        return 0

    lax.fori_loop(0, 128, emit, 0, unroll=2)


def synth(recv, low, up, ints):
    return pl.pallas_call(
        synth_kernel,
        grid_spec=pltpu.PrefetchScalarGridSpec(
            num_scalar_prefetch=1,
            grid=(1,),
            in_specs=[
                pl.BlockSpec((8, 512, 128), lambda g, b: (0, 0, 0)),
                pl.BlockSpec((2, LMAX, HALF), lambda g, b: (b[0], 0, 0)),
                pl.BlockSpec((2, LMAX // 2, HALF), lambda g, b: (b[0], 0, 0)),
                pl.BlockSpec((256, 512), lambda g, b: (0, 0)),
            ],
            out_specs=pl.BlockSpec((128, 96, 128), lambda g, b: (0, 0, 0)),
            scratch_shapes=[pltpu.VMEM((8, HALF, 128), f32), pltpu.VMEM((8 * 2 * 96 * 8, 128), f32)],
        ),
        out_shape=jax.ShapeDtypeStruct((128, 96, 128), bf16),
        compiler_params=params(),
        cost_estimate=pl.CostEstimate(flops=2000000000, bytes_accessed=7000000, transcendentals=0),
        name="synth",
    )(ints, recv, low, up, radial_matrix())


def grid_kernel(
    ints_ref, sines_ref, recv_ref, vel_ref, t_ref, d_ref, a_ref, out_ref,
    ke, ko, l0e, l0o, l1e, l1o, se, so, ze, zo, ue, uo, oe, oo,
):
    step = pl.program_id(0)
    top = lax.broadcasted_iota(jnp.int32, (8, 128), 0) < 4

    def gather(u, _):
        a = recv_ref[2 * u].astype(f32)
        b = recv_ref[2 * u + 1].astype(f32)
        for t in range(4):
            at = a[8 * t : 8 * t + 8]
            bt = b[8 * t : 8 * t + 8]
            row = pl.multiple_of(t * 512 + 8 * u, 8)
            ke[pl.ds(row, 8), :] = jnp.where(top, at, pltpu.roll(bt, 4, 0))
            ko[pl.ds(row, 8), :] = jnp.where(top, pltpu.roll(at, 4, 0), bt)
        return 0

    lax.fori_loop(0, 64, gather, 0, unroll=4)
    for t in range(4):
        for src, zero, one in ((ke, l0e, l1e), (ko, l0o, l1o)):
            turned = src[512 * t : 512 * t + 512, :].T.astype(bf16)
            for j in range(4):
                row = (t * 4 + j) * 16
                zero[row : row + 16, :] = turned[32 * j : 32 * j + 16]
                one[row : row + 16, :] = turned[32 * j + 16 : 32 * j + 32]
    se[...] = jnp.dot(l1e[...], t_ref[0:512, :], preferred_element_type=f32)
    so[...] = jnp.dot(l1o[...], t_ref[512:1024, :], preferred_element_type=f32)
    ze[...] = jnp.dot(l0e[...], d_ref[0:512, :], preferred_element_type=f32)
    zo[...] = jnp.dot(l0o[...], d_ref[512:1024, :], preferred_element_type=f32)
    south = ints_ref[3]

    def flux(j, _):
        local = jnp.where(south == 1, 15 - j, j)
        sine = sines_ref[step * 16 + j]
        rows = pl.ds(pl.multiple_of(j * 16, 16), 16)
        for b in range(3):
            lo = slice(256 * b, 256 * b + 256)
            hi = slice(NH + 256 * b, NH + 256 * b + 256)
            v0 = vel_ref[0, local, :, lo].astype(f32) * sine
            v1 = vel_ref[1, local, :, lo].astype(f32)
            w0 = vel_ref[0, local, :, hi].astype(f32) * sine
            w1 = vel_ref[1, local, :, hi].astype(f32)
            s_e = se[rows, lo]
            s_o = so[rows, lo]
            z_e = ze[rows, lo]
            z_o = zo[rows, lo]
            near = v0 * (s_e + s_o) + v1 * (z_e + z_o)
            far = w0 * (s_e - s_o) + w1 * (z_e - z_o)
            ue[rows, lo] = (near + far).astype(bf16)
            uo[rows, lo] = (near - far).astype(bf16)
        return 0

    lax.fori_loop(0, 16, flux, 0)
    for dst, src, first in ((oe, ue, 0), (oo, uo, 512)):
        res = lax.dot_general(src[...], a_ref[first : first + 512, :], NT, preferred_element_type=f32)
        for ta in range(4):
            dst[ta] = res[:, 128 * ta : 128 * ta + 128]
    for ta in range(4):
        for ip in range(8):
            i0 = pl.ds(2 * ip, 16, stride=16)
            i1 = pl.ds(2 * ip + 1, 16, stride=16)
            parts = swap_chunks(oe[ta, i0, :], oo[ta, i0, :], oe[ta, i1, :], oo[ta, i1, :])
            for al in range(4):
                out_ref[4 * ta + al, :, 128 * ip : 128 * ip + 128] = parts[al].astype(bf16)


def grid_stage(recv, velocity, tables, ints, sines):
    whole = pl.BlockSpec((1024, NH), lambda g, *_: (0, 0), pipeline_mode=pl.Buffered(1))

    def latitude_block(g, ints, sines):
        return (0, jnp.where(ints[3] == 1, 2 - g, g), 0, 0)

    wide = [pltpu.VMEM((256, NH), f32)] * 4
    return pl.pallas_call(
        grid_kernel,
        grid_spec=pltpu.PrefetchScalarGridSpec(
            num_scalar_prefetch=2,
            grid=(3,),
            in_specs=[
                pl.BlockSpec((128, 32, 128), lambda g, *_: (0, g, 0)),
                pl.BlockSpec((2, 16, 16, NLON), latitude_block),
                whole,
                whole,
                whole,
            ],
            out_specs=pl.BlockSpec((16, 16, 1024), lambda g, *_: (0, g, 0)),
            scratch_shapes=[pltpu.VMEM((2048, 128), f32)] * 2
            + [pltpu.VMEM((256, 512), bf16)] * 4
            + wide
            + [pltpu.VMEM((256, NH), bf16)] * 2
            + [pltpu.VMEM((4, 256, 128), f32)] * 2,
        ),
        out_shape=jax.ShapeDtypeStruct((16, 48, 1024), bf16),
        compiler_params=params(),
        cost_estimate=pl.CostEstimate(flops=3700000000, bytes_accessed=14000000, transcendentals=0),
        name="grid",
    )(ints, sines, recv, velocity, *tables)


def analyse_body(par_ref, recv_ref, low_ref, up_ref, out_low, out_up, plus, minus, part_p, part_m):
    step = pl.program_id(0)

    @pl.when(step == 0)
    def _():
        for t in range(8):
            lanes = slice(128 * t, 128 * t + 128)
            for a in range(8):
                north = recv_ref[a, :, lanes].astype(f32)
                south = recv_ref[15 - a, :, lanes].astype(f32)
                part_p[48 * a : 48 * a + 48, :] = north + south
                part_m[48 * a : 48 * a + 48, :] = north - south
            for b in range(3):
                rows = slice(128 * b, 128 * b + 128)
                plus[b, lanes, :] = part_p[rows, :].T
                minus[b, lanes, :] = part_m[rows, :].T

    for q in range(2):
        pair = step * 2 + q
        h0 = par_ref[pair]
        for lu in range(2):
            h = h0 if lu == 0 else 1 - h0
            base = h * 32 + pair * 2
            left = jnp.concatenate(
                [
                    jnp.concatenate([ref[b, pl.ds(base + c, 16, stride=64), :] for b in range(3)], 1)
                    for ref in (plus, minus)
                    for c in range(2)
                ],
                0,
            ).astype(bf16)
            table = low_ref[q] if lu == 0 else up_ref[q]
            res = lax.dot_general(left, table, NT, preferred_element_type=f32)
            degree = lax.broadcasted_iota(jnp.int32, (32, res.shape[1]), 1)
            res = jnp.where((degree + h) % 2 == 0, res[0:32], res[32:64]).astype(bf16)
            if lu == 0:
                out_low[q, 0] = res[0:16]
                out_low[q, 1] = res[16:32]
            else:
                zero = jnp.zeros((16, 256), bf16)
                for c in range(2):
                    out_up[q, c, :, 0:256] = zero
                    out_up[q, c, :, 256:512] = res[16 * c : 16 * c + 16]


def analyse(recv, low, up, parity):
    out = pl.BlockSpec((2, 2, 16, LMAX), lambda g, *_: (g, 0, 0, 0))
    return pl.pallas_call(
        analyse_body,
        grid_spec=pltpu.PrefetchScalarGridSpec(
            num_scalar_prefetch=1,
            grid=(8,),
            in_specs=[
                pl.BlockSpec((16, 48, 1024), lambda g, *_: (0, 0, 0), pipeline_mode=pl.Buffered(1)),
                pl.BlockSpec((2, LMAX, HALF), lambda g, *_: (g, 0, 0)),
                pl.BlockSpec((2, LMAX // 2, HALF), lambda g, *_: (g, 0, 0)),
            ],
            out_specs=[out, out],
            scratch_shapes=[
                pltpu.VMEM((3, 1024, 128), f32),
                pltpu.VMEM((3, 1024, 128), f32),
                pltpu.VMEM((HALF, 128), f32),
                pltpu.VMEM((HALF, 128), f32),
            ],
        ),
        out_shape=[jax.ShapeDtypeStruct((16, 2, 16, LMAX), bf16)] * 2,
        compiler_params=params(),
        cost_estimate=pl.CostEstimate(flops=1200000000, bytes_accessed=12000000, transcendentals=0),
        name="analyse",
    )(parity, recv, low, up)


def local(source_coeffs, inverses, velocity, order_slots):
    rad_index = lax.axis_index("rad")
    ang_index = lax.axis_index("ang")
    blocks = order_slots.reshape(16, 2, 16)
    lower = blocks[:, 0]
    upper = blocks[:, 1]
    is_even = lower % 2 == 0
    even = jnp.where(is_even, lower, upper)
    odd = jnp.where(is_even, upper, lower)
    by_source = [v.reshape(16, 8, 2).transpose(1, 0, 2).reshape(256) for v in (even, odd)]
    synth_orders = jnp.concatenate(by_source)
    analyse_orders = jnp.concatenate([even.reshape(256), odd.reshape(256)])
    my_orders = lax.dynamic_slice_in_dim(order_slots, ang_index * 32, 32, 0)
    parity = my_orders[:16] % 2
    south = (ang_index >= 8).astype(jnp.int32)
    ints = jnp.concatenate(
        [rad_index[None].astype(jnp.int32), lax.dynamic_slice_in_dim(parity, rad_index * 2, 2, 0), south[None]]
    )
    position = jnp.arange(48, dtype=jnp.int32)
    latitude = ang_index * 48 + jnp.where(south == 1, 47 - position, position)
    sines = jnp.sin((latitude.astype(f32) + 0.5) * (math.pi / NLAT))

    sent = solve(source_coeffs, inverses, my_orders, rad_index)
    coeffs = lax.all_to_all(sent, "rad", 0, 0, tiled=True)
    low, up = legendre_tables(my_orders)
    tables = fourier_tables(synth_orders, analyse_orders)
    fields = synth(coeffs, low, up, ints)
    fields = lax.all_to_all(fields, ("rad", "ang"), 0, 0, tiled=True)
    fourier = grid_stage(fields, velocity, tables, ints, sines)
    fourier = lax.all_to_all(fourier, "ang", 0, 0, tiled=True)
    out_low, out_up = analyse(fourier, low, up, parity)
    return jnp.concatenate([out_low, out_up], 0)


def solution(mesh):
    in_specs = (P("ang", "rad", None, None), P("rad", None, None), P(None, "ang", "rad", None), P())
    out_specs = P("ang", None, "rad", None)
    return jax.shard_map(local, mesh=mesh, in_specs=in_specs, out_specs=out_specs, check_vma=False)
```

time: 2020 us -> 164 us (0.08); the launches traced: 2000 us -> 163 us
  other arithmetic: 900 us -> 16 us
  local copies, waits for them, and re-layouts: 543 us -> 10.7 us
  loops' own time: 375 us -> 0 us
  matrix products: 88.5 us -> 0 us
  Pallas kernels: 0 us -> 76.7 us
  waiting for transfers between devices: 40.7 us -> 16.1 us
    dynamic_update_slice x512 -> x0, other arithmetic: 397 us -> none  [legendre_rows(): lax.scan(advance, (zero_field, zero_field, log_start), jnp.arange(degree_...]
    another operation x1 -> x0, loops' own time: 375 us -> none  [legendre_rows(): lax.scan(advance, (zero_field, zero_field, log_start), jnp.arange(degree_...]
    or x512 -> x0, other arithmetic: 356 us -> none  [advance(): previous = jnp.where(before | starting, 0.0, prev_one)]
    dynamic_slice x512 -> x1, local copies, waits for them, and re-layouts: 338 us -> 0.08 us  [local(): lax.dynamic_slice_in_dim(parity, rad_index * 2, 2, 0)]
    dot_general x6 -> x0, matrix products: 88.5 us -> none  [the longest x1 28.2 us: local(): jnp.einsum('sfcli,lsj->sfcij', radial, legendre, preferred_element_type=j...]
    cos x514 -> x0, other arithmetic: 79.9 us -> none  [the longest x512 63.9 us: legendre_rows(): cosines = jnp.cos(colatitude)[None, :]]
    all_to_all x7 -> x0, local copies, waits for them, and re-layouts: 78.5 us -> none  [the longest x2 46 us: local(): lax.all_to_all(sending, 'ang', split_axis=4, concat_axis=0, tiled=True)]
    pallas_call x0 -> x6, Pallas kernels: none -> 76.7 us  [the longest x1 27.6 us: legendre_tables(): pl.pallas_call(legendre_kernel, grid_spec=pltpu.PrefetchScalarGridSpec(nu...]
  transfers between devices with their start and end apart: 2 -> 2, of which waited for: 1 -> 1; matrix products, arithmetic and copies ran while one was open for 62% -> 12% of each run, Pallas kernels for 0% -> 21%
where the time goes in v1:
time: 164 us; the launch traced here: 163 us
  Pallas kernels  76.7 us (47%)
  blocking collectives  27.1 us (17%)
  starting transfers between devices  16.3 us (10%)
  waiting for transfers between devices  16.1 us (10%)
  other arithmetic  16 us (10%)
  local copies, waits for them, and re-layouts  10.7 us (7%)
    pallas_call x1, Pallas kernels, legendre_tables(): pl.pallas_call(legendre_kernel, grid_spec=pltpu.PrefetchScalarGridSpec(nu...  27.6 us
    all_to_all x1, blocking collectives, local(): fourier = lax.all_to_all(fourier, 'ang', 0, 0, tiled=True)  27.1 us
    all_to_all x1, waiting for transfers between devices, local(): fields = lax.all_to_all(fields, ('rad', 'ang'), 0, 0, tiled=True)  16.1 us
    pallas_call x1, Pallas kernels, grid_stage(): pl.pallas_call(grid_kernel, grid_spec=pltpu.PrefetchScalarGridSpec(num_sc...  13.8 us
    pallas_call x1, Pallas kernels, synth(): pl.pallas_call(synth_kernel, grid_spec=pltpu.PrefetchScalarGridSpec(num_s...  11.7 us
    all_to_all x1, starting transfers between devices, local(): fields = lax.all_to_all(fields, ('rad', 'ang'), 0, 0, tiled=True)  11.6 us
    sin x2, other arithmetic, phase_rows(): return (jnp.cos(near), jnp.sin(near), jnp.cos(far), jnp.sin(far))  10.9 us
    pallas_call x1, Pallas kernels, analyse(): pl.pallas_call(analyse_body, grid_spec=pltpu.PrefetchScalarGridSpec(num_s...  10.8 us
  transfers between devices with their start and end apart: 2, of which 1 were waited for; matrix products, arithmetic and copies ran while one was open for 12% of the time, Pallas kernels for 21%

profile of v1, /device:TPU:0, one launch (start us, length us, event | category | flops | bytes accessed | tf_op | source)
XLA Modules:
  0.0 163.0 jit_solution(17749256376578362319)
XLA Ops:
  0.0 0.8 compare_select_fusion.2
  0.8 0.7 broadcast_in_dim.64.order_ref
  1.5 6.0 %solve.1 = bf16[8,512,128]{2,1,0:T(8,128)(2,1)} custom-call(s32[1]{0:T(128)} %bitcast.2.base_ref, bf16[32,128,128]{2,1,0:T(8,128)(2,1)} %bitcast.10, bf16[64,128,128]{2,1,0:T(8,128)(2,1)} %inv_ref.1, s32[64,128]{1,0:T(8,128)} %broadcast_in_dim.64.order_ref), custom_call_target="tpu_custom_call" | custom-call | flops 134217728 | bytes 4194304 | tf_op jit(solution)/shard_map/solve/pallas_call | solution.py:100
  7.5 4.7 %all-to-all-start = ((bf16[8,512,128]{2,1,0:T(8,128)(2,1)}), bf16[8,512,128]{2,1,0:T(8,128)(2,1)S(1)}, u32[]{:S(2)}, u32[]{:S(2)}) async-start(bf16[8,512,128]{2,1,0:T(8,128)(2,1)} %solve.1), calls=%async_computation | async-start | bytes 2097152 | tf_op jit(solution)/shard_map/all_to_all | solution.py:534
  12.4 0.7 gather_fusion
  13.1 0.7 multiply_add_fusion.log_ref
  13.8 0.7 broadcast_in_dim.65.m_ref
  14.5 27.6 %legendre.1 = (bf16[16,512,384]{2,1,0:T(8,128)(2,1)}, bf16[16,256,384]{2,1,0:T(8,128)(2,1)}) custom-call(f32[512]{0:T(512)} %constant.120.clone.c1_ref, f32[512]{0:T(512)} %constant.121.clone.c2_ref, f32[32,128]{1,0:T(8,128)} %broadcast_in_dim.65.m_ref, f32[16,384]{1,0:T(8,128)} %constant.117.clone.x_ref, f32[32,384]{1,0:T(8,128)} %multiply_add_fusion.log_ref), custom_call_target="tpu_custom_call" | custom-call | flops 60000000 | bytes 12582912 | tf_op jit(solution)/shard_map/legendre/pallas_call | solution.py:194
  42.0 0.6 pad_add_fusion.2.ints_ref
  42.7 1.0 copy-done.2
  43.6 11.7 %synth.1 = bf16[128,96,128]{2,1,0:T(8,128)(2,1)} custom-call(s32[4]{0:T(128)} %pad_add_fusion.2.ints_ref, bf16[8,512,128]{2,1,0:T(8,128)(2,1)} %copy-done.2, bf16[16,512,384]{2,1,0:T(8,128)(2,1)} %get-tuple-element.12.low_ref, bf16[16,256,384]{2,1,0:T(8,128)(2,1)} %get-tuple-element.13.up_ref, bf16[256,512]{1,0:T(8,128)(2,1)} %constant.124.mat_ref), custom_call_target="tpu_custom_call" | custom-call | flops 2000000000 | bytes 7000000 | tf_op jit(solution)/shard_map/synth/pallas_call | solution.py:318
  55.4 11.6 %all-to-all-start.1 = ((bf16[128,96,128]{2,1,0:T(8,128)(2,1)}), bf16[128,96,128]{2,1,0:T(8,128)(2,1)S(1)}, u32[]{:S(2)}, u32[]{:S(2)}) async-start(bf16[128,96,128]{2,1,0:T(8,128)(2,1)} %synth.1), calls=%async_computation.1 | async-start | bytes 6291456 | tf_op jit(solution)/shard_map/all_to_all | solution.py:538
  67.4 0.1 copy.21
  67.5 0.1 reshape.64
  67.8 0.1 reshape.65
  68.1 0.2 mul.125
  68.4 0.2 mul.136
  68.6 0.2 add.104
  68.9 1.0 copy.24
  70.0 1.0 copy.23
  71.0 6.3 %fusion.6 = (f32[1024,128]{1,0:T(8,128)}, f32[1024,128]{1,0:T(8,128)}, f32[1024,128]{1,0:T(8,128)}, f32[1024,128]{1,0:T(8,128)}) fusion(s32[1024]{0:T(1024)S(1)} %mul.136, s32[1024]{0:T(1024)S(1)} %add.104, s32[1024]{0:T(1024)S(1)} %mul.125), kind=kLoop, calls=%fused_computation.11 | loop fusion | flops 2621440 | bytes 2109440 | tf_op jit(solution)/shard_map/sin | solution.py:239
  77.3 4.6 %multiply_sine_fusion = (f32[1024,8]{1,0:T(8,128)}, f32[1024,8]{1,0:T(8,128)}, f32[1024,8]{1,0:T(8,128)}, f32[1024,8]{1,0:T(8,128)}) fusion(f32[1024,8]{1,0:T(8,128)S(1)} %copy-done.3, f32[1024,8]{1,0:T(8,128)S(1)} %copy-done.4), kind=kLoop, calls=%fused_computation.20 | loop fusion | flops 16384 | bytes 196608 | tf_op jit(solution)/shard_map/sin | solution.py:239
  81.9 1.0 broadcast_in_dim.72.mw
  82.9 1.0 broadcast_in_dim.71.w
  83.9 6.9 %tables.1 = (bf16[1024,768]{1,0:T(8,128)(2,1)}, bf16[1024,768]{1,0:T(8,128)(2,1)}, bf16[1024,768]{1,0:T(8,128)(2,1)}) custom-call(f32[1024,128]{1,0:T(8,128)} %get-tuple-element.35.nc, f32[1024,128]{1,0:T(8,128)} %get-tuple-element.36.ns, f32[1024,8]{1,0:T(8,128)} %get-tuple-element.43.fc, f32[1024,8]{1,0:T(8,128)} %get-tuple-element.44.fs, ...), custom_call_target="tpu_custom_call" | custom-call | flops 8000000 | bytes 8000000 | tf_op jit(solution)/shard_map/tables/pallas_call | solution.py:263
  90.8 0.6 multiply_sine_fusion.2.sines_ref
  91.4 16.1 %all-to-all-done.1.recv_ref = bf16[128,96,128]{2,1,0:T(8,128)(2,1)S(1)} async-done(((bf16[128,96,128]{2,1,0:T(8,128)(2,1)}), bf16[128,96,128]{2,1,0:T(8,128)(2,1)S(1)}, u32[]{:S(2)}, u32[]{:S(2)}) %all-to-all-start.1) | async-done | bytes 3145760 | tf_op jit(solution)/shard_map/all_to_all | solution.py:538
  107.4 1.7 %copy-done.1 = bf16[128,96,128]{2,1,0:T(8,128)(2,1)} copy-done((bf16[128,96,128]{2,1,0:T(8,128)(2,1)}, bf16[128,96,128]{2,1,0:T(8,128)(2,1)S(1)}, u32[]{:S(2)}) %copy-start.1) | copy-done | bytes 3145752
  109.1 13.8 %grid.1 = bf16[16,48,1024]{2,1,0:T(8,128)(2,1)} custom-call(s32[4]{0:T(128)} %pad_add_fusion.2.ints_ref, f32[48]{0:T(128)} %multiply_sine_fusion.2.sines_ref, bf16[128,96,128]{2,1,0:T(8,128)(2,1)} %copy-done.1, bf16[2,48,16,1536]{3,2,1,0:T(8,128)(2,1)} %vel_ref.1, bf16[1024,768]{1,0:T(8,128)(2,1)} %get-tuple-element.14.t_ref, ...), custom_call_target="tpu_custom_call" | custom-call | flops 3700000000 | bytes 14000000 | tf_op jit(solution)/shard_map/grid/pallas_call | solution.py:413
  122.9 27.1 %all_to_all.15.recv_ref = bf16[16,48,1024]{2,1,0:T(8,128)(2,1)} all-to-all(bf16[16,48,1024]{2,1,0:T(8,128)(2,1)} %grid.1), channel_id=1, replica_groups=mesh['rad'=8,'ang'=16] {'ang'}, dimensions={0} | all-to-all | bytes 3145728 | tf_op jit(solution)/shard_map/all_to_all | solution.py:540
  149.9 10.8 %analyse.1 = (bf16[16,2,16,512]{3,2,1,0:T(8,128)(2,1)}, bf16[16,2,16,512]{3,2,1,0:T(8,128)(2,1)}) custom-call(s32[16]{0:T(128)} %copy-done.7, bf16[16,48,1024]{2,1,0:T(8,128)(2,1)} %all_to_all.15.recv_ref, bf16[16,512,384]{2,1,0:T(8,128)(2,1)} %get-tuple-element.12.low_ref, bf16[16,256,384]{2,1,0:T(8,128)(2,1)} %get-tuple-element.13.up_ref), custom_call_target="tpu_custom_call" | custom-call | flops 1200000000 | bytes 12000000 | tf_op jit(solution)/shard_map/analyse/pallas_call | solution.py:486
  160.7 2.3 %pad_maximum_fusion = bf16[32,2,16,512]{3,2,1,0:T(8,128)(2,1)} fusion(bf16[16,2,16,512]{3,2,1,0:T(8,128)(2,1)} %get-tuple-element.18, bf16[16,2,16,512]{3,2,1,0:T(8,128)(2,1)} %get-tuple-element.17), kind=kLoop, calls=%fused_computation.1 | loop fusion | flops 524288 | bytes 2097152 | tf_op jit(solution)/shard_map/concatenate | solution.py:542
  (40 shorter events, 1.2 us)
Async XLA Ops:
  7.5 4.8 %copy-start = (f32[512]{0:T(512)S(1)}, f32[512]{0:T(512)}, u32[]{:S(2)}) copy-start(f32[512]{0:T(512)} %constant.118.clone) | copy-start | bytes 6148
  7.5 5.6 %copy-start.6 = (f32[384]{0:T(512)S(1)}, f32[384]{0:T(512)}, u32[]{:S(2)}) copy-start(f32[384]{0:T(512)} %constant.119.clone) | copy-start | bytes 4612
  7.5 35.1 %all-to-all-start = ((bf16[8,512,128]{2,1,0:T(8,128)(2,1)}), bf16[8,512,128]{2,1,0:T(8,128)(2,1)S(1)}, u32[]{:S(2)}, u32[]{:S(2)}) async-start(bf16[8,512,128]{2,1,0:T(8,128)(2,1)} %solve.1), calls=%async_computation | async-start | bytes 2097152 | tf_op jit(solution)/shard_map/all_to_all | solution.py:534
  12.3 43.1 %copy-start.7 = (s32[16]{0:T(128)}, s32[16]{0:T(128)S(1)}, u32[]{:S(2)}) copy-start(s32[16]{0:T(128)S(1)} %and_select_fusion.3.par_ref) | copy-start | bytes 196
  42.7 1.0 copy-start.2
  55.4 11.6 %copy-start.5 = (s32[512]{0:T(512)S(1)}, s32[512]{0:T(512)}, u32[]{:S(2)}) copy-start(s32[512]{0:T(512)} %param.15) | copy-start | bytes 6148
  55.4 52.1 %all-to-all-start.1 = ((bf16[128,96,128]{2,1,0:T(8,128)(2,1)}), bf16[128,96,128]{2,1,0:T(8,128)(2,1)S(1)}, u32[]{:S(2)}, u32[]{:S(2)}) async-start(bf16[128,96,128]{2,1,0:T(8,128)(2,1)} %synth.1), calls=%async_computation.1 | async-start | bytes 6291456 | tf_op jit(solution)/shard_map/all_to_all | solution.py:538
  71.0 6.4 %copy-start.3 = (f32[1024,8]{1,0:T(8,128)S(1)}, f32[1024,8]{1,0:T(8,128)}, u32[]{:S(2)}) copy-start(f32[1024,8]{1,0:T(8,128)} %copy.24) | copy-start | bytes 98308
  71.0 6.4 %copy-start.4 = (f32[1024,8]{1,0:T(8,128)S(1)}, f32[1024,8]{1,0:T(8,128)}, u32[]{:S(2)}) copy-start(f32[1024,8]{1,0:T(8,128)} %copy.23) | copy-start | bytes 98308
  107.4 1.7 %copy-start.1 = (bf16[128,96,128]{2,1,0:T(8,128)(2,1)}, bf16[128,96,128]{2,1,0:T(8,128)(2,1)S(1)}, u32[]{:S(2)}) copy-start(bf16[128,96,128]{2,1,0:T(8,128)(2,1)S(1)} %all-to-all-done.1.recv_ref) | copy-start | bytes 9437188

commit v2 on v1

--- a/solution.py
+++ b/solution.py
@@ -1,3 +1,4 @@
+import functools
 import math
 
 import jax
@@ -117,7 +118,9 @@
     )(jnp.reshape(rad_index * 64, (1,)), src, inverses, order)
 
 
-def legendre_kernel(c1_ref, c2_ref, m_ref, x_ref, log_ref, low_ref, up_ref, p1, p2, lg, bp, tile):
+def legendre_kernel(groups, c1_ref, c2_ref, m_ref, x_ref, log_ref, *refs):
+    outs = refs[: len(groups)]
+    p1, p2, lg, bp, tile = refs[len(groups) :]
     step = pl.program_id(0)
 
     @pl.when(step == 0)
@@ -127,8 +130,8 @@
         bp[...] = jnp.zeros(bp.shape, f32)
         lg[...] = log_ref[...]
 
-    def run(half, out_ref):
-        rows = slice(half * 16, half * 16 + 16)
+    def run(start, count, out_ref):
+        rows = slice(start, start + count)
         m = m_ref[rows, :]
         m2 = m * m
         lanes = [slice(128 * t, 128 * t + 128) for t in range(3)]
@@ -148,10 +151,10 @@
                 below = d * r * c2_ref[l]
                 seed = jnp.where(m == lf, 1.0, 0.0)
                 for t in range(3):
-                    new = (a * x_ref[:, lanes[t]]) * cur[t] - ab * prev[t] + seed
+                    new = (a * x_ref[0:count, lanes[t]]) * cur[t] - ab * prev[t] + seed
                     prev[t] = cur[t]
                     cur[t] = new
-                    tile[t, pl.ds(local, 16, stride=32), :] = new * scale[t]
+                    tile[t, pl.ds(local, count, stride=32), :] = new * scale[t]
             for t in range(3):
                 big = jnp.abs(cur[t]) > grow_bound
                 factor = jnp.where(big, 1.0 / grow_bound, 1.0)
@@ -172,18 +175,19 @@
             p2[rows, lanes[t]] = prev[t]
             lg[rows, lanes[t]] = logs[t]
         bp[rows, :] = below
-        for s in range(16):
+        for s in range(out_ref.shape[0]):
             for t in range(3):
                 out_ref[s, :, lanes[t]] = tile[t, s * 32 : s * 32 + 32, :].astype(bf16)
 
-    run(0, low_ref)
-
-    @pl.when(step >= 8)
-    def _():
-        run(1, up_ref)
-
-
-def legendre_tables(orders):
+    for (start, count, _, first), out_ref in zip(groups, outs):
+        if first == 0:
+            run(start, count, out_ref)
+        else:
+            pl.when(step >= first)(lambda: run(start, count, out_ref))
+
+
+def legendre_tables(orders, groups, name):
+    total = orders.shape[0]
     l = np.arange(LMAX, dtype=np.float64)
     root = np.sqrt(np.maximum(4.0 * l * l - 1.0, 1.0))
     t = (np.arange(HALF) + 0.5) * (math.pi / NLAT)
@@ -191,39 +195,37 @@
     x = jnp.asarray(np.broadcast_to(np.cos(t), (16, HALF)), f32)
     mf = orders.astype(f32)
     logs = jnp.take(jnp.asarray(gammas, f32), orders)[:, None] + mf[:, None] * jnp.asarray(np.log(np.sin(t)), f32)[None]
+
+    def out_spec(slots, first):
+        return pl.BlockSpec((slots, 32, HALF), lambda g, *_: (0, jnp.maximum(g - first, 0), 0))
+
     return pl.pallas_call(
-        legendre_kernel,
+        functools.partial(legendre_kernel, groups),
         grid_spec=pltpu.PrefetchScalarGridSpec(
             num_scalar_prefetch=2,
             grid=(16,),
             in_specs=[
-                pl.BlockSpec((32, 128), lambda g, *_: (0, 0)),
+                pl.BlockSpec((total, 128), lambda g, *_: (0, 0)),
                 pl.BlockSpec((16, HALF), lambda g, *_: (0, 0)),
-                pl.BlockSpec((32, HALF), lambda g, *_: (0, 0)),
-            ],
-            out_specs=[
-                pl.BlockSpec((16, 32, HALF), lambda g, *_: (0, g, 0)),
-                pl.BlockSpec((16, 32, HALF), lambda g, *_: (0, jnp.maximum(g - 8, 0), 0)),
-            ],
+                pl.BlockSpec((total, HALF), lambda g, *_: (0, 0)),
+            ],
+            out_specs=[out_spec(slots, first) for _, _, slots, first in groups],
             scratch_shapes=[
-                pltpu.VMEM((32, HALF), f32),
-                pltpu.VMEM((32, HALF), f32),
-                pltpu.VMEM((32, HALF), f32),
-                pltpu.VMEM((32, 128), f32),
+                pltpu.VMEM((total, HALF), f32),
+                pltpu.VMEM((total, HALF), f32),
+                pltpu.VMEM((total, HALF), f32),
+                pltpu.VMEM((total, 128), f32),
                 pltpu.VMEM((3, 512, 128), f32),
             ],
         ),
-        out_shape=[
-            jax.ShapeDtypeStruct((16, LMAX, HALF), bf16),
-            jax.ShapeDtypeStruct((16, LMAX // 2, HALF), bf16),
-        ],
+        out_shape=[jax.ShapeDtypeStruct((slots, LMAX - 32 * first, HALF), bf16) for _, _, slots, first in groups],
         compiler_params=params(),
-        cost_estimate=pl.CostEstimate(flops=60000000, bytes_accessed=12582912, transcendentals=100000),
-        name="legendre",
+        cost_estimate=pl.CostEstimate(flops=2000000 * total, bytes_accessed=400000 * total, transcendentals=3000 * total),
+        name=name,
     )(
         jnp.asarray(root, f32),
         jnp.asarray(1.0 / root, f32),
-        jnp.broadcast_to(mf[:, None], (32, 128)),
+        jnp.broadcast_to(mf[:, None], (total, 128)),
         x,
         logs,
     )
@@ -239,40 +241,39 @@
     return (jnp.cos(near), jnp.sin(near), jnp.cos(far), jnp.sin(far))
 
 
-def table_kernel(nc, ns, fc, fs, w, mw, anc, ans, afc, afs, t_ref, d_ref, a_ref):
+def table_kernel(nc, ns, fc, fs, w, t_ref, d_ref, a_ref):
     scale = (2.0 * math.pi / NLON) * (math.pi / NLAT)
+    weight = w[:, 0:1]
+    turn = w[:, 1:2]
     for b in range(6):
         lanes = slice(128 * b, 128 * b + 128)
         cosine = fc[:, b : b + 1] * nc[...] - fs[:, b : b + 1] * ns[...]
         sine = fs[:, b : b + 1] * nc[...] + fc[:, b : b + 1] * ns[...]
-        t_ref[:, lanes] = (w[...] * cosine).astype(bf16)
-        d_ref[:, lanes] = (mw[...] * sine).astype(bf16)
-        a_ref[:, lanes] = (scale * (afc[:, b : b + 1] * anc[...] - afs[:, b : b + 1] * ans[...])).astype(bf16)
-
-
-def fourier_tables(synth_orders, analyse_orders):
-    synth = phase_rows(synth_orders)
-    analyse = phase_rows(analyse_orders)
-    m = jnp.repeat(synth_orders, 2).astype(f32)
+        t_ref[:, lanes] = (weight * cosine).astype(bf16)
+        d_ref[:, lanes] = (turn * sine).astype(bf16)
+        a_ref[:, lanes] = (scale * cosine).astype(bf16)
+
+
+def fourier_tables(rows, orders):
+    m = jnp.repeat(orders, 2).astype(f32)
     w = jnp.where(m == 0.0, 1.0, 2.0)
-    w2 = jnp.broadcast_to(w[:, None], (1024, 128))
-    mw2 = jnp.broadcast_to((-m * w)[:, None], (1024, 128))
+    weights = jnp.stack([w, -m * w] * 4, 1)
     near = pl.BlockSpec((256, 128), lambda g: (g, 0))
     far = pl.BlockSpec((256, 8), lambda g: (g, 0))
     out = pl.BlockSpec((256, NH), lambda g: (g, 0))
     return pl.pallas_call(
         table_kernel,
         grid=(4,),
-        in_specs=[near, near, far, far, near, near, near, near, far, far],
+        in_specs=[near, near, far, far, far],
         out_specs=[out, out, out],
         out_shape=[jax.ShapeDtypeStruct((1024, NH), bf16)] * 3,
         compiler_params=params(),
         cost_estimate=pl.CostEstimate(flops=8000000, bytes_accessed=8000000, transcendentals=0),
         name="tables",
-    )(*synth, w2, mw2, *analyse)
-
-
-def synth_kernel(ints_ref, recv_ref, low_ref, up_ref, mat_ref, out_ref, ns, scr):
+    )(*rows, weights)
+
+
+def synth_kernel(ints_ref, recv_ref, leg_ref, mat_ref, out_ref, ns, scr):
     mat = mat_ref[...]
     for lu in range(2):
         for q in range(2):
@@ -289,7 +290,7 @@
             degree = lax.broadcasted_iota(jnp.int32, rad.shape, 0)
             sign = (1 - 2 * ((degree + h) % 2)).astype(f32)
             both = jnp.concatenate([rad.astype(bf16), (rad * sign).astype(bf16)], 1)
-            table = low_ref[q] if lu == 0 else up_ref[q]
+            table = leg_ref[lu * 2 + q, 64 * first : LMAX, :]
             wave = lax.dot_general(table, both, TN, preferred_element_type=f32)
             for tile in range(8):
                 ns[tile] = wave[:, 128 * tile : 128 * tile + 128]
@@ -303,8 +304,8 @@
                             scr[pl.ds(base + h * 4, 96, stride=8), :] = parts[rl]
 
     def emit(i, _):
-        r = i // 16
-        a = i % 16
+        r = i % 8
+        a = i // 8
         half = a // 8
         north = jnp.where(half == 0, a, 15 - a)
         start = pl.multiple_of(((r * 2 + half) * 96 + north * 12) * 8, 32)
@@ -314,7 +315,7 @@
     lax.fori_loop(0, 128, emit, 0, unroll=2)
 
 
-def synth(recv, low, up, ints):
+def synth(recv, table, ints):
     return pl.pallas_call(
         synth_kernel,
         grid_spec=pltpu.PrefetchScalarGridSpec(
@@ -322,8 +323,7 @@
             grid=(1,),
             in_specs=[
                 pl.BlockSpec((8, 512, 128), lambda g, b: (0, 0, 0)),
-                pl.BlockSpec((2, LMAX, HALF), lambda g, b: (b[0], 0, 0)),
-                pl.BlockSpec((2, LMAX // 2, HALF), lambda g, b: (b[0], 0, 0)),
+                pl.BlockSpec((4, LMAX, HALF), lambda g, b: (0, 0, 0)),
                 pl.BlockSpec((256, 512), lambda g, b: (0, 0)),
             ],
             out_specs=pl.BlockSpec((128, 96, 128), lambda g, b: (0, 0, 0)),
@@ -333,7 +333,7 @@
         compiler_params=params(),
         cost_estimate=pl.CostEstimate(flops=2000000000, bytes_accessed=7000000, transcendentals=0),
         name="synth",
-    )(ints, recv, low, up, radial_matrix())
+    )(ints, recv, table, radial_matrix())
 
 
 def grid_kernel(
@@ -436,7 +436,7 @@
     )(ints, sines, recv, velocity, *tables)
 
 
-def analyse_body(par_ref, recv_ref, low_ref, up_ref, out_low, out_up, plus, minus, part_p, part_m):
+def analyse_body(par_ref, recv_ref, low_ref, up_ref, out_ref, plus, minus, part_p, part_m):
     step = pl.program_id(0)
 
     @pl.when(step == 0)
@@ -472,17 +472,17 @@
             degree = lax.broadcasted_iota(jnp.int32, (32, res.shape[1]), 1)
             res = jnp.where((degree + h) % 2 == 0, res[0:32], res[32:64]).astype(bf16)
             if lu == 0:
-                out_low[q, 0] = res[0:16]
-                out_low[q, 1] = res[16:32]
+                out_ref[0, q, 0] = res[0:16]
+                out_ref[0, q, 1] = res[16:32]
             else:
                 zero = jnp.zeros((16, 256), bf16)
                 for c in range(2):
-                    out_up[q, c, :, 0:256] = zero
-                    out_up[q, c, :, 256:512] = res[16 * c : 16 * c + 16]
+                    out_ref[1, q, c, :, 0:256] = zero
+                    out_ref[1, q, c, :, 256:512] = res[16 * c : 16 * c + 16]
 
 
 def analyse(recv, low, up, parity):
-    out = pl.BlockSpec((2, 2, 16, LMAX), lambda g, *_: (g, 0, 0, 0))
+    out = pl.BlockSpec((2, 2, 2, 16, LMAX), lambda g, *_: (0, g, 0, 0, 0))
     return pl.pallas_call(
         analyse_body,
         grid_spec=pltpu.PrefetchScalarGridSpec(
@@ -493,7 +493,7 @@
                 pl.BlockSpec((2, LMAX, HALF), lambda g, *_: (g, 0, 0)),
                 pl.BlockSpec((2, LMAX // 2, HALF), lambda g, *_: (g, 0, 0)),
             ],
-            out_specs=[out, out],
+            out_specs=out,
             scratch_shapes=[
                 pltpu.VMEM((3, 1024, 128), f32),
                 pltpu.VMEM((3, 1024, 128), f32),
@@ -501,7 +501,7 @@
                 pltpu.VMEM((HALF, 128), f32),
             ],
         ),
-        out_shape=[jax.ShapeDtypeStruct((16, 2, 16, LMAX), bf16)] * 2,
+        out_shape=jax.ShapeDtypeStruct((2, 16, 2, 16, LMAX), bf16),
         compiler_params=params(),
         cost_estimate=pl.CostEstimate(flops=1200000000, bytes_accessed=12000000, transcendentals=0),
         name="analyse",
@@ -517,9 +517,7 @@
     is_even = lower % 2 == 0
     even = jnp.where(is_even, lower, upper)
     odd = jnp.where(is_even, upper, lower)
-    by_source = [v.reshape(16, 8, 2).transpose(1, 0, 2).reshape(256) for v in (even, odd)]
-    synth_orders = jnp.concatenate(by_source)
-    analyse_orders = jnp.concatenate([even.reshape(256), odd.reshape(256)])
+    fourier_orders = jnp.concatenate([even.reshape(256), odd.reshape(256)])
     my_orders = lax.dynamic_slice_in_dim(order_slots, ang_index * 32, 32, 0)
     parity = my_orders[:16] % 2
     south = (ang_index >= 8).astype(jnp.int32)
@@ -531,15 +529,22 @@
     sines = jnp.sin((latitude.astype(f32) + 0.5) * (math.pi / NLAT))
 
     sent = solve(source_coeffs, inverses, my_orders, rad_index)
+    early, sent = lax.optimization_barrier((fourier_orders, sent))
     coeffs = lax.all_to_all(sent, "rad", 0, 0, tiled=True)
-    low, up = legendre_tables(my_orders)
-    tables = fourier_tables(synth_orders, analyse_orders)
-    fields = synth(coeffs, low, up, ints)
-    fields = lax.all_to_all(fields, ("rad", "ang"), 0, 0, tiled=True)
+    pairs = [lax.dynamic_slice_in_dim(v, rad_index * 2, 2, 0) for v in (my_orders[:16], my_orders[16:])]
+    own_orders = jnp.concatenate(pairs * 2)
+    (own,) = legendre_tables(own_orders, ((0, 8, 4, 0),), "legendre_own")
+    rows = phase_rows(early)
+    coeffs, own, rows = lax.optimization_barrier((coeffs, own, rows))
+    fields = synth(coeffs, own, ints)
+    fields, late, rows = lax.optimization_barrier((fields, my_orders, rows))
+    fields = lax.all_to_all(fields, ("ang", "rad"), 0, 0, tiled=True)
+    low, up = legendre_tables(late, ((0, 16, 16, 0), (16, 16, 16, 8)), "legendre")
+    tables = fourier_tables(rows, fourier_orders)
+    fields, low, up, tables = lax.optimization_barrier((fields, low, up, tables))
     fourier = grid_stage(fields, velocity, tables, ints, sines)
     fourier = lax.all_to_all(fourier, "ang", 0, 0, tiled=True)
-    out_low, out_up = analyse(fourier, low, up, parity)
-    return jnp.concatenate([out_low, out_up], 0)
+    return analyse(fourier, low, up, parity).reshape(32, 2, 16, LMAX)
 
 
 def solution(mesh):

time: 164 us -> 155 us (0.945)
  waiting for transfers between devices: 16.1 us -> 3.73 us
  Pallas kernels: 76.7 us -> 86.9 us
  other arithmetic: 16 us -> 9.8 us
    all_to_all x1, waiting for transfers between devices: 16.1 us -> 3.72 us  [local(): fields = lax.all_to_all(fields, ('ang', 'rad'), 0, 0, tiled=True)]
    pallas_call x2 -> x3, Pallas kernels: 34.4 us -> 44.5 us  [the longest x2 38.7 us: legendre_tables(): pl.pallas_call(functools.partial(legendre_kernel, groups), grid_spec=pltp...]
    sin x2, other arithmetic: 10.9 us -> 6.95 us  [phase_rows(): return (jnp.cos(near), jnp.sin(near), jnp.cos(far), jnp.sin(far))]
    concatenate x3 -> x1, other arithmetic: 2.28 us -> 0.01 us  [local(): fourier_orders = jnp.concatenate([even.reshape(256), odd.reshape(256)])]
    convert_element_type x2 -> x0, local copies, waits for them, and re-layouts: 2.04 us -> none  [phase_rows(): far = far.astype(f32) * (2.0 * math.pi / NLON)]
  transfers between devices with their start and end apart: 2 -> 2, of which waited for: 1 -> 1; matrix products, arithmetic and copies ran while one was open for 12% -> 10% of each run, Pallas kernels for 21% -> 29%
where the time goes in v2:
time: 155 us; the launch traced here: 154 us
  Pallas kernels  86.9 us (56%)
  blocking collectives  26.9 us (17%)
  starting transfers between devices  16.3 us (11%)
  local copies, waits for them, and re-layouts  10.4 us (7%)
  other arithmetic  9.8 us (6%)
  waiting for transfers between devices  3.73 us (2%)
    pallas_call x2, Pallas kernels, legendre_tables(): pl.pallas_call(functools.partial(legendre_kernel, groups), grid_spec=pltp...  38.7 us
    all_to_all x1, blocking collectives, local(): fourier = lax.all_to_all(fourier, 'ang', 0, 0, tiled=True)  26.9 us
    pallas_call x1, Pallas kernels, grid_stage(): pl.pallas_call(grid_kernel, grid_spec=pltpu.PrefetchScalarGridSpec(num_sc...  13.7 us
    pallas_call x1, Pallas kernels, synth(): pl.pallas_call(synth_kernel, grid_spec=pltpu.PrefetchScalarGridSpec(num_s...  11.9 us
    all_to_all x1, starting transfers between devices, local(): fields = lax.all_to_all(fields, ('ang', 'rad'), 0, 0, tiled=True)  11.6 us
    pallas_call x1, Pallas kernels, analyse(): pl.pallas_call(analyse_body, grid_spec=pltpu.PrefetchScalarGridSpec(num_s...  10.8 us
    sin x2, other arithmetic, phase_rows(): return (jnp.cos(near), jnp.sin(near), jnp.cos(far), jnp.sin(far))  6.95 us
    pallas_call x1, Pallas kernels, solve(): pl.pallas_call(solve_kernel, grid_spec=pltpu.PrefetchScalarGridSpec(num_s...  6 us
  transfers between devices with their start and end apart: 2, of which 1 were waited for; matrix products, arithmetic and copies ran while one was open for 10% of the time, Pallas kernels for 29%

profile of v2, /device:TPU:0, one launch (start us, length us, event | category | flops | bytes accessed | tf_op | source)
XLA Modules:
  0.0 154.2 jit_solution(15267695213457020903)
XLA Ops:
  0.0 0.8 reshape.323
  0.8 0.8 dynamic_slice.12
  1.9 0.7 broadcast_in_dim.62.order_ref
  2.5 6.0 %solve.1 = bf16[8,512,128]{2,1,0:T(8,128)(2,1)} custom-call(s32[1]{0:T(128)} %bitcast.2.base_ref, bf16[32,128,128]{2,1,0:T(8,128)(2,1)} %bitcast.11, bf16[64,128,128]{2,1,0:T(8,128)(2,1)} %inv_ref.1, s32[64,128]{1,0:T(8,128)} %broadcast_in_dim.62.order_ref), custom_call_target="tpu_custom_call" | custom-call | flops 134217728 | bytes 4194304 | tf_op jit(solution)/shard_map/solve/pallas_call | solution.py:101
  8.6 4.7 %all-to-all-start = ((bf16[8,512,128]{2,1,0:T(8,128)(2,1)}), bf16[8,512,128]{2,1,0:T(8,128)(2,1)S(1)}, u32[]{:S(2)}, u32[]{:S(2)}) async-start(bf16[8,512,128]{2,1,0:T(8,128)(2,1)} %solve.1), calls=%async_computation | async-start | bytes 2097152 | tf_op jit(solution)/shard_map/all_to_all | solution.py:533
  13.8 0.6 gather_fusion
  14.6 0.2 add.110
  14.9 0.2 mul.112
  15.1 0.7 multiply_add_fusion.1.log_ref
  15.7 0.7 broadcast_in_dim.63.m_ref
  16.4 11.1 %legendre_own.1.leg_ref = bf16[4,512,384]{2,1,0:T(8,128)(2,1)} custom-call(f32[512]{0:T(512)} %constant.124.clone.c1_ref, f32[512]{0:T(512)} %constant.125.clone.c2_ref, f32[8,128]{1,0:T(8,128)} %broadcast_in_dim.63.m_ref, f32[16,384]{1,0:T(8,128)} %constant.121.clone.x_ref, f32[8,384]{1,0:T(8,128)} %multiply_add_fusion.1.log_ref), custom_call_target="tpu_custom_call" | custom-call | flops 16000000 | bytes 3200000 | tf_op jit(solution)/shard_map/legendre_own/pallas_call | solution.py:202
  27.5 0.6 pad_add_fusion.1.ints_ref
  28.1 3.3 %fusion.6 = (f32[1024,8]{1,0:T(8,128)}, f32[1024,8]{1,0:T(8,128)}) fusion(s32[1024]{0:T(1024)S(1)} %mul.112, s32[8]{0:T(128)S(1)} %iota_multiply_fusion), kind=kLoop, calls=%fused_computation.11 | loop fusion | flops 73728 | bytes 69664 | tf_op jit(solution)/shard_map/sin | solution.py:241
  31.4 3.7 %fusion.10 = (f32[1024,128]{1,0:T(8,128)}, f32[1024,128]{1,0:T(8,128)}) fusion(s32[1024]{0:T(1024)S(1)} %add.110, s32[1024]{0:T(1024)S(1)} %mul.112), kind=kLoop, calls=%fused_computation.16 | loop fusion | flops 1310720 | bytes 1056768 | tf_op jit(solution)/shard_map/sin | solution.py:241
  35.1 1.0 copy-done.2
  36.1 11.9 %synth.1 = bf16[128,96,128]{2,1,0:T(8,128)(2,1)} custom-call(s32[4]{0:T(128)} %pad_add_fusion.1.ints_ref, bf16[8,512,128]{2,1,0:T(8,128)(2,1)} %copy-done.2, bf16[4,512,384]{2,1,0:T(8,128)(2,1)} %legendre_own.1.leg_ref, bf16[256,512]{1,0:T(8,128)(2,1)} %constant.128.mat_ref), custom_call_target="tpu_custom_call" | custom-call | flops 2000000000 | bytes 7000000 | tf_op jit(solution)/shard_map/synth/pallas_call | solution.py:319
  48.0 11.6 %all-to-all-start.1 = ((bf16[128,96,128]{2,1,0:T(8,128)(2,1)}), bf16[128,96,128]{2,1,0:T(8,128)(2,1)S(1)}, u32[]{:S(2)}, u32[]{:S(2)}) async-start(bf16[128,96,128]{2,1,0:T(8,128)(2,1)} %synth.1), calls=%async_computation.1 | async-start | bytes 6291456 | tf_op jit(solution)/shard_map/all_to_all | solution.py:541
  59.7 0.2 neg.15
  59.9 0.1 broadcast_in_dim.70
  60.0 0.2 select_n.125
  60.3 1.0 copy.25.w
  61.3 0.6 multiply_sine_fusion.sines_ref
  61.9 0.7 gather_fusion.1
  62.6 5.8 %tables.1 = (bf16[1024,768]{1,0:T(8,128)(2,1)}, bf16[1024,768]{1,0:T(8,128)(2,1)}, bf16[1024,768]{1,0:T(8,128)(2,1)}) custom-call(f32[1024,128]{1,0:T(8,128)} %get-tuple-element.42.nc, f32[1024,128]{1,0:T(8,128)} %get-tuple-element.43.ns, f32[1024,8]{1,0:T(8,128)} %get-tuple-element.44.fc, f32[1024,8]{1,0:T(8,128)} %get-tuple-element.45.fs, f32[1024,8]{1,0:T(8,128)} %copy.25.w), custom_call_target="tpu_custom_call" | custom-call | flops 8000000 | bytes 8000000 | tf_op jit(solution)/shard_map/tables/pallas_call | solution.py:264
  68.4 0.7 multiply_add_fusion.log_ref
  69.1 0.7 broadcast_in_dim.65.m_ref
  69.8 27.6 %legendre.1 = (bf16[16,512,384]{2,1,0:T(8,128)(2,1)}, bf16[16,256,384]{2,1,0:T(8,128)(2,1)}) custom-call(f32[512]{0:T(512)} %constant.124.clone.c1_ref, f32[512]{0:T(512)} %constant.125.clone.c2_ref, f32[32,128]{1,0:T(8,128)} %broadcast_in_dim.65.m_ref, f32[16,384]{1,0:T(8,128)} %constant.121.clone.x_ref, f32[32,384]{1,0:T(8,128)} %multiply_add_fusion.log_ref), custom_call_target="tpu_custom_call" | custom-call | flops 64000000 | bytes 12800000 | tf_op jit(solution)/shard_map/legendre/pallas_call | solution.py:202
  97.4 3.7 %all-to-all-done.1.recv_ref = bf16[128,96,128]{2,1,0:T(8,128)(2,1)S(1)} async-done(((bf16[128,96,128]{2,1,0:T(8,128)(2,1)}), bf16[128,96,128]{2,1,0:T(8,128)(2,1)S(1)}, u32[]{:S(2)}, u32[]{:S(2)}) %all-to-all-start.1) | async-done | bytes 3145760 | tf_op jit(solution)/shard_map/all_to_all | solution.py:541
  101.1 1.7 %copy-done.1 = bf16[128,96,128]{2,1,0:T(8,128)(2,1)} copy-done((bf16[128,96,128]{2,1,0:T(8,128)(2,1)}, bf16[128,96,128]{2,1,0:T(8,128)(2,1)S(1)}, u32[]{:S(2)}) %copy-start.1) | copy-done | bytes 3145752
  102.8 13.7 %grid.1 = bf16[16,48,1024]{2,1,0:T(8,128)(2,1)} custom-call(s32[4]{0:T(128)} %pad_add_fusion.1.ints_ref, f32[48]{0:T(128)} %multiply_sine_fusion.sines_ref, bf16[128,96,128]{2,1,0:T(8,128)(2,1)} %copy-done.1, bf16[2,48,16,1536]{3,2,1,0:T(8,128)(2,1)} %vel_ref.1, bf16[1024,768]{1,0:T(8,128)(2,1)} %get-tuple-element.50.t_ref, ...), custom_call_target="tpu_custom_call" | custom-call | flops 3700000000 | bytes 14000000 | tf_op jit(solution)/shard_map/grid/pallas_call | solution.py:413
  116.5 26.9 %all_to_all.15.recv_ref = bf16[16,48,1024]{2,1,0:T(8,128)(2,1)} all-to-all(bf16[16,48,1024]{2,1,0:T(8,128)(2,1)} %grid.1), channel_id=1, replica_groups=mesh['rad'=8,'ang'=16] {'ang'}, dimensions={0} | all-to-all | bytes 3145728 | tf_op jit(solution)/shard_map/all_to_all | solution.py:546
  143.5 10.8 %analyse.1 = bf16[2,16,2,16,512]{4,3,2,1,0:T(8,128)(2,1)} custom-call(s32[16]{0:T(128)} %copy-done.4, bf16[16,48,1024]{2,1,0:T(8,128)(2,1)} %all_to_all.15.recv_ref, bf16[16,512,384]{2,1,0:T(8,128)(2,1)} %get-tuple-element.53.low_ref, bf16[16,256,384]{2,1,0:T(8,128)(2,1)} %get-tuple-element.54.up_ref), custom_call_target="tpu_custom_call" | custom-call | flops 1200000000 | bytes 12000000 | tf_op jit(solution)/shard_map/analyse/pallas_call | solution.py:486
  (37 shorter events, 1.3 us)
Async XLA Ops:
  8.5 5.3 %copy-start = (f32[512]{0:T(512)S(1)}, f32[512]{0:T(512)}, u32[]{:S(2)}) copy-start(f32[512]{0:T(512)} %constant.122.clone) | copy-start | bytes 6148
  8.5 6.5 %copy-start.3 = (f32[384]{0:T(512)S(1)}, f32[384]{0:T(512)}, u32[]{:S(2)}) copy-start(f32[384]{0:T(512)} %constant.123.clone) | copy-start | bytes 4612
  8.6 26.5 %all-to-all-start = ((bf16[8,512,128]{2,1,0:T(8,128)(2,1)}), bf16[8,512,128]{2,1,0:T(8,128)(2,1)S(1)}, u32[]{:S(2)}, u32[]{:S(2)}) async-start(bf16[8,512,128]{2,1,0:T(8,128)(2,1)} %solve.1), calls=%async_computation | async-start | bytes 2097152 | tf_op jit(solution)/shard_map/all_to_all | solution.py:533
  13.3 18.0 %copy-start.4 = (s32[16]{0:T(128)}, s32[16]{0:T(128)S(1)}, u32[]{:S(2)}) copy-start(s32[16]{0:T(128)S(1)} %get-tuple-element.70.par_ref) | copy-start | bytes 196
  35.1 1.0 copy-start.2
  48.0 53.1 %all-to-all-start.1 = ((bf16[128,96,128]{2,1,0:T(8,128)(2,1)}), bf16[128,96,128]{2,1,0:T(8,128)(2,1)S(1)}, u32[]{:S(2)}, u32[]{:S(2)}) async-start(bf16[128,96,128]{2,1,0:T(8,128)(2,1)} %synth.1), calls=%async_computation.1 | async-start | bytes 6291456 | tf_op jit(solution)/shard_map/all_to_all | solution.py:541
  101.1 1.7 %copy-start.1 = (bf16[128,96,128]{2,1,0:T(8,128)(2,1)}, bf16[128,96,128]{2,1,0:T(8,128)(2,1)S(1)}, u32[]{:S(2)}) copy-start(bf16[128,96,128]{2,1,0:T(8,128)(2,1)S(1)} %all-to-all-done.1.recv_ref) | copy-start | bytes 9437188

commit v3 on v2

--- a/solution.py
+++ b/solution.py
@@ -31,10 +31,10 @@
     value = np.cos(k * u[None])
     slope = k * np.sin(k * u[None]) / np.sin(u)[None] * (2.0 / (1.0 - inner_radius))
     both = np.stack([value / r, slope + 3.0 * value / r], 0)
-    both = both.reshape(2, K, 8, 16).transpose(1, 2, 0, 3).reshape(K, 256)
-    out = np.zeros((2, K, 2, 256))
-    out[0, :, 0] = both
-    out[1, :, 1] = both
+    both = both.reshape(2, K, 8, 16).transpose(1, 2, 0, 3).reshape(K, 8, 32)
+    out = np.zeros((2, K, 8, 2, 32))
+    out[0, :, :, 0] = both
+    out[1, :, :, 1] = both
     return jnp.asarray(out.reshape(256, 512), f32).astype(bf16)
 
 
@@ -65,7 +65,7 @@
     @pl.when(step == 0)
     def _():
         def widen(s, _):
-            wide[pl.ds(pl.multiple_of(s * 128, 128), 128), :] = src_ref[s].astype(f32)
+            wide[pl.ds(pl.multiple_of(s * 136, 8), 128), :] = src_ref[s].astype(f32)
             return 0
 
         lax.fori_loop(0, 32, widen, 0, unroll=4)
@@ -74,12 +74,12 @@
 
     def degree(i, _):
         row = step * block + i
-        x0 = wide[pl.ds(2 * row, 32, stride=128), :]
-        x1 = wide[pl.ds(2 * row + 1, 32, stride=128), :]
+        x0 = wide[pl.ds(2 * row, 32, stride=136), :]
+        x1 = wide[pl.ds(2 * row + 1, 32, stride=136), :]
         x = jnp.concatenate([x0, x1], 0).astype(bf16)
         y = lax.dot_general(x, inv_ref[i], NT, preferred_element_type=f32)
         y = jnp.where(order <= base_ref[0] + row, y, 0.0)
-        acc[pl.ds(row, 64, stride=64), :] = y
+        acc[pl.ds(row, 64, stride=72), :] = y
         return 0
 
     lax.fori_loop(0, block, degree, 0, unroll=8)
@@ -92,7 +92,7 @@
                     for c in range(2):
                         plane = c * 32 + lu * 16 + 2 * r + q
                         row = (lu * 4 + q * 2 + c) * 64
-                        out_ref[r, row : row + 64, :] = acc[plane * 64 : plane * 64 + 64, :].astype(bf16)
+                        out_ref[r, row : row + 64, :] = acc[plane * 72 : plane * 72 + 64, :].astype(bf16)
 
 
 def solve(source, inverses, orders, rad_index):
@@ -109,7 +109,7 @@
                 pl.BlockSpec((64, 128), lambda g, b: (0, 0)),
             ],
             out_specs=pl.BlockSpec((8, 512, 128), lambda g, b: (0, 0, 0)),
-            scratch_shapes=[pltpu.VMEM((4096, 128), f32), pltpu.VMEM((4096, 128), f32)],
+            scratch_shapes=[pltpu.VMEM((32 * 136, 128), f32), pltpu.VMEM((64 * 72, 128), f32)],
         ),
         out_shape=jax.ShapeDtypeStruct((8, 512, 128), bf16),
         compiler_params=params(),
@@ -154,7 +154,7 @@
                     new = (a * x_ref[0:count, lanes[t]]) * cur[t] - ab * prev[t] + seed
                     prev[t] = cur[t]
                     cur[t] = new
-                    tile[t, pl.ds(local, count, stride=32), :] = new * scale[t]
+                    tile[t, pl.ds(local, count, stride=40), :] = new * scale[t]
             for t in range(3):
                 big = jnp.abs(cur[t]) > grow_bound
                 factor = jnp.where(big, 1.0 / grow_bound, 1.0)
@@ -177,7 +177,7 @@
         bp[rows, :] = below
         for s in range(out_ref.shape[0]):
             for t in range(3):
-                out_ref[s, :, lanes[t]] = tile[t, s * 32 : s * 32 + 32, :].astype(bf16)
+                out_ref[s, :, lanes[t]] = tile[t, s * 40 : s * 40 + 32, :].astype(bf16)
 
     for (start, count, _, first), out_ref in zip(groups, outs):
         if first == 0:
@@ -215,7 +215,7 @@
                 pltpu.VMEM((total, HALF), f32),
                 pltpu.VMEM((total, HALF), f32),
                 pltpu.VMEM((total, 128), f32),
-                pltpu.VMEM((3, 512, 128), f32),
+                pltpu.VMEM((3, 640, 128), f32),
             ],
         ),
         out_shape=[jax.ShapeDtypeStruct((slots, LMAX - 32 * first, HALF), bf16) for _, _, slots, first in groups],
@@ -232,48 +232,59 @@
 
 
 def phase_rows(orders):
-    m = jnp.repeat(orders, 2)[:, None]
-    c = jnp.tile(jnp.asarray([0, NLON // 4], jnp.int32), orders.shape[0])[:, None]
-    near = (m * jnp.arange(128, dtype=jnp.int32)[None] + c) % NLON
+    m = orders[:, None]
+    near = (m * jnp.arange(128, dtype=jnp.int32)[None]) % NLON
     far = (m * (128 * jnp.arange(8, dtype=jnp.int32))[None]) % NLON
     near = near.astype(f32) * (2.0 * math.pi / NLON)
     far = far.astype(f32) * (2.0 * math.pi / NLON)
-    return (jnp.cos(near), jnp.sin(near), jnp.cos(far), jnp.sin(far))
+    m = orders.astype(f32)
+    w = jnp.where(m == 0.0, 1.0, 2.0)
+    weights = jnp.stack([w, -m * w] * 4, 1)
+    return (jnp.cos(near), jnp.sin(near), jnp.cos(far), jnp.sin(far), weights)
 
 
 def table_kernel(nc, ns, fc, fs, w, t_ref, d_ref, a_ref):
     scale = (2.0 * math.pi / NLON) * (math.pi / NLAT)
-    weight = w[:, 0:1]
-    turn = w[:, 1:2]
     for b in range(6):
         lanes = slice(128 * b, 128 * b + 128)
-        cosine = fc[:, b : b + 1] * nc[...] - fs[:, b : b + 1] * ns[...]
-        sine = fs[:, b : b + 1] * nc[...] + fc[:, b : b + 1] * ns[...]
-        t_ref[:, lanes] = (weight * cosine).astype(bf16)
-        d_ref[:, lanes] = (turn * sine).astype(bf16)
-        a_ref[:, lanes] = (scale * cosine).astype(bf16)
-
-
-def fourier_tables(rows, orders):
-    m = jnp.repeat(orders, 2).astype(f32)
-    w = jnp.where(m == 0.0, 1.0, 2.0)
-    weights = jnp.stack([w, -m * w] * 4, 1)
+        parts = []
+        for q in range(2):
+            rows = slice(128 * q, 128 * q + 128)
+            far_cos = fc[rows, b : b + 1]
+            far_sin = fs[rows, b : b + 1]
+            cosine = far_cos * nc[rows, :] - far_sin * ns[rows, :]
+            sine = far_sin * nc[rows, :] + far_cos * ns[rows, :]
+            weight = w[rows, 0:1]
+            turn = w[rows, 1:2]
+            first = slice(256 * q, 256 * q + 128)
+            second = slice(256 * q + 128, 256 * q + 256)
+            t_ref[first, lanes] = (weight * cosine).astype(bf16)
+            t_ref[second, lanes] = (-weight * sine).astype(bf16)
+            d_ref[first, lanes] = (turn * sine).astype(bf16)
+            d_ref[second, lanes] = (turn * cosine).astype(bf16)
+            parts += [scale * cosine, -scale * sine]
+        for a in range(16):
+            rows = jnp.concatenate([v[8 * a : 8 * a + 8] for v in parts], 0)
+            a_ref[32 * a : 32 * a + 32, lanes] = rows.astype(bf16)
+
+
+def fourier_tables(rows):
     near = pl.BlockSpec((256, 128), lambda g: (g, 0))
     far = pl.BlockSpec((256, 8), lambda g: (g, 0))
-    out = pl.BlockSpec((256, NH), lambda g: (g, 0))
+    out = pl.BlockSpec((512, NH), lambda g: (g, 0))
     return pl.pallas_call(
         table_kernel,
-        grid=(4,),
+        grid=(2,),
         in_specs=[near, near, far, far, far],
         out_specs=[out, out, out],
         out_shape=[jax.ShapeDtypeStruct((1024, NH), bf16)] * 3,
         compiler_params=params(),
         cost_estimate=pl.CostEstimate(flops=8000000, bytes_accessed=8000000, transcendentals=0),
         name="tables",
-    )(*rows, weights)
-
-
-def synth_kernel(ints_ref, recv_ref, leg_ref, mat_ref, out_ref, ns, scr):
+    )(*rows)
+
+
+def synth_kernel(ints_ref, recv_ref, leg_ref, mat_ref, out_ref, ns):
     mat = mat_ref[...]
     for lu in range(2):
         for q in range(2):
@@ -293,26 +304,23 @@
             table = leg_ref[lu * 2 + q, 64 * first : LMAX, :]
             wave = lax.dot_general(table, both, TN, preferred_element_type=f32)
             for tile in range(8):
-                ns[tile] = wave[:, 128 * tile : 128 * tile + 128]
-            for half in range(2):
-                for c in range(2):
-                    for rh in range(2):
-                        tile = half * 4 + c * 2 + rh
-                        parts = swap_chunks(*[ns[tile, pl.ds(j, 96, stride=4), :] for j in range(4)])
-                        for rl in range(4):
-                            base = (((rh * 4 + rl) * 2 + half) * 96) * 8 + q * 2 + c
-                            scr[pl.ds(base + h * 4, 96, stride=8), :] = parts[rl]
-
-    def emit(i, _):
-        r = i % 8
-        a = i // 8
-        half = a // 8
-        north = jnp.where(half == 0, a, 15 - a)
-        start = pl.multiple_of(((r * 2 + half) * 96 + north * 12) * 8, 32)
-        out_ref[i] = scr[pl.ds(start, 96), :].astype(bf16)
-        return 0
-
-    lax.fori_loop(0, 128, emit, 0, unroll=2)
+                ns[lu * 2 + q, tile] = wave[:, 128 * tile : 128 * tile + 128]
+    low = lax.broadcasted_iota(jnp.int32, (HALF, 128), 1) < 64
+    for h in range(2):
+        first, second = [(ints_ref[1 + q] if h == 0 else 1 - ints_ref[1 + q]) * 2 + q for q in range(2)]
+        for half in range(2):
+            for rh in range(4):
+                v0 = ns[first, half * 4 + rh]
+                v1 = ns[second, half * 4 + rh]
+                parts = (
+                    jnp.where(low, v0, pltpu.roll(v1, 64, 1)),
+                    jnp.where(low, pltpu.roll(v0, 64, 1), v1),
+                )
+                for rl in range(2):
+                    for north in range(8):
+                        a = north if half == 0 else 15 - north
+                        rows = parts[rl][48 * north : 48 * north + 48]
+                        out_ref[a * 8 + rh * 2 + rl, 48 * h : 48 * h + 48, :] = rows.astype(bf16)
 
 
 def synth(recv, table, ints):
@@ -327,7 +335,7 @@
                 pl.BlockSpec((256, 512), lambda g, b: (0, 0)),
             ],
             out_specs=pl.BlockSpec((128, 96, 128), lambda g, b: (0, 0, 0)),
-            scratch_shapes=[pltpu.VMEM((8, HALF, 128), f32), pltpu.VMEM((8 * 2 * 96 * 8, 128), f32)],
+            scratch_shapes=[pltpu.VMEM((4, 8, HALF, 128), f32)],
         ),
         out_shape=jax.ShapeDtypeStruct((128, 96, 128), bf16),
         compiler_params=params(),
@@ -338,30 +346,24 @@
 
 def grid_kernel(
     ints_ref, sines_ref, recv_ref, vel_ref, t_ref, d_ref, a_ref, out_ref,
-    ke, ko, l0e, l0o, l1e, l1o, se, so, ze, zo, ue, uo, oe, oo,
+    wide, l0e, l0o, l1e, l1o, se, so, ze, zo, ue, uo, oe, oo,
 ):
     step = pl.program_id(0)
-    top = lax.broadcasted_iota(jnp.int32, (8, 128), 0) < 4
-
-    def gather(u, _):
-        a = recv_ref[2 * u].astype(f32)
-        b = recv_ref[2 * u + 1].astype(f32)
-        for t in range(4):
-            at = a[8 * t : 8 * t + 8]
-            bt = b[8 * t : 8 * t + 8]
-            row = pl.multiple_of(t * 512 + 8 * u, 8)
-            ke[pl.ds(row, 8), :] = jnp.where(top, at, pltpu.roll(bt, 4, 0))
-            ko[pl.ds(row, 8), :] = jnp.where(top, pltpu.roll(at, 4, 0), bt)
+
+    def widen(u, _):
+        row = pl.multiple_of(u * 40, 8)
+        wide[pl.ds(row, 16), :] = recv_ref[u, 0].astype(f32)
+        wide[pl.ds(row + 16, 16), :] = recv_ref[u, 1].astype(f32)
         return 0
 
-    lax.fori_loop(0, 64, gather, 0, unroll=4)
-    for t in range(4):
-        for src, zero, one in ((ke, l0e, l1e), (ko, l0o, l1o)):
-            turned = src[512 * t : 512 * t + 512, :].T.astype(bf16)
-            for j in range(4):
-                row = (t * 4 + j) * 16
-                zero[row : row + 16, :] = turned[32 * j : 32 * j + 16]
-                one[row : row + 16, :] = turned[32 * j + 16 : 32 * j + 32]
+    lax.fori_loop(0, 128, widen, 0, unroll=8)
+    for j in range(16):
+        for h, zero, one in ((0, l0e, l1e), (1, l0o, l1o)):
+            turned = wide[pl.ds(h * 16 + j, 128, stride=40), :].astype(bf16).T
+            for k in range(4):
+                lanes = slice(128 * k, 128 * k + 128)
+                zero[16 * j : 16 * j + 16, lanes] = turned[32 * k : 32 * k + 16]
+                one[16 * j : 16 * j + 16, lanes] = turned[32 * k + 16 : 32 * k + 32]
     se[...] = jnp.dot(l1e[...], t_ref[0:512, :], preferred_element_type=f32)
     so[...] = jnp.dot(l1o[...], t_ref[512:1024, :], preferred_element_type=f32)
     ze[...] = jnp.dot(l0e[...], d_ref[0:512, :], preferred_element_type=f32)
@@ -393,11 +395,12 @@
     for dst, src, first in ((oe, ue, 0), (oo, uo, 512)):
         res = lax.dot_general(src[...], a_ref[first : first + 512, :], NT, preferred_element_type=f32)
         for ta in range(4):
-            dst[ta] = res[:, 128 * ta : 128 * ta + 128]
+            for j in range(16):
+                dst[ta, 24 * j : 24 * j + 16, :] = res[16 * j : 16 * j + 16, 128 * ta : 128 * ta + 128]
     for ta in range(4):
         for ip in range(8):
-            i0 = pl.ds(2 * ip, 16, stride=16)
-            i1 = pl.ds(2 * ip + 1, 16, stride=16)
+            i0 = pl.ds(2 * ip, 16, stride=24)
+            i1 = pl.ds(2 * ip + 1, 16, stride=24)
             parts = swap_chunks(oe[ta, i0, :], oo[ta, i0, :], oe[ta, i1, :], oo[ta, i1, :])
             for al in range(4):
                 out_ref[4 * ta + al, :, 128 * ip : 128 * ip + 128] = parts[al].astype(bf16)
@@ -416,24 +419,24 @@
             num_scalar_prefetch=2,
             grid=(3,),
             in_specs=[
-                pl.BlockSpec((128, 32, 128), lambda g, *_: (0, g, 0)),
+                pl.BlockSpec((128, 2, 16, 128), lambda g, *_: (0, 0, g, 0)),
                 pl.BlockSpec((2, 16, 16, NLON), latitude_block),
                 whole,
                 whole,
                 whole,
             ],
             out_specs=pl.BlockSpec((16, 16, 1024), lambda g, *_: (0, g, 0)),
-            scratch_shapes=[pltpu.VMEM((2048, 128), f32)] * 2
+            scratch_shapes=[pltpu.VMEM((128 * 40, 128), f32)]
             + [pltpu.VMEM((256, 512), bf16)] * 4
             + wide
             + [pltpu.VMEM((256, NH), bf16)] * 2
-            + [pltpu.VMEM((4, 256, 128), f32)] * 2,
+            + [pltpu.VMEM((4, 384, 128), f32)] * 2,
         ),
         out_shape=jax.ShapeDtypeStruct((16, 48, 1024), bf16),
         compiler_params=params(),
         cost_estimate=pl.CostEstimate(flops=3700000000, bytes_accessed=14000000, transcendentals=0),
         name="grid",
-    )(ints, sines, recv, velocity, *tables)
+    )(ints, sines, recv.reshape(128, 2, 48, 128), velocity, *tables)
 
 
 def analyse_body(par_ref, recv_ref, low_ref, up_ref, out_ref, plus, minus, part_p, part_m):
@@ -450,18 +453,20 @@
                 part_m[48 * a : 48 * a + 48, :] = north - south
             for b in range(3):
                 rows = slice(128 * b, 128 * b + 128)
-                plus[b, lanes, :] = part_p[rows, :].T
-                minus[b, lanes, :] = part_m[rows, :].T
+                for part, dst in ((part_p, plus), (part_m, minus)):
+                    turned = part[rows, :].T
+                    dst[b, 144 * t : 144 * t + 64, :] = turned[0:64]
+                    dst[b, 144 * t + 72 : 144 * t + 136, :] = turned[64:128]
 
     for q in range(2):
         pair = step * 2 + q
         h0 = par_ref[pair]
         for lu in range(2):
             h = h0 if lu == 0 else 1 - h0
-            base = h * 32 + pair * 2
+            base = h * 32 + q * 16 + step
             left = jnp.concatenate(
                 [
-                    jnp.concatenate([ref[b, pl.ds(base + c, 16, stride=64), :] for b in range(3)], 1)
+                    jnp.concatenate([ref[b, pl.ds(base + 8 * c, 16, stride=72), :] for b in range(3)], 1)
                     for ref in (plus, minus)
                     for c in range(2)
                 ],
@@ -495,8 +500,8 @@
             ],
             out_specs=out,
             scratch_shapes=[
-                pltpu.VMEM((3, 1024, 128), f32),
-                pltpu.VMEM((3, 1024, 128), f32),
+                pltpu.VMEM((3, 1152, 128), f32),
+                pltpu.VMEM((3, 1152, 128), f32),
                 pltpu.VMEM((HALF, 128), f32),
                 pltpu.VMEM((HALF, 128), f32),
             ],
@@ -517,7 +522,8 @@
     is_even = lower % 2 == 0
     even = jnp.where(is_even, lower, upper)
     odd = jnp.where(is_even, upper, lower)
-    fourier_orders = jnp.concatenate([even.reshape(256), odd.reshape(256)])
+    by_parity = [v.reshape(16, 8, 2).transpose(2, 0, 1).reshape(256) for v in (even, odd)]
+    fourier_orders = jnp.concatenate(by_parity)
     my_orders = lax.dynamic_slice_in_dim(order_slots, ang_index * 32, 32, 0)
     parity = my_orders[:16] % 2
     south = (ang_index >= 8).astype(jnp.int32)
@@ -529,18 +535,15 @@
     sines = jnp.sin((latitude.astype(f32) + 0.5) * (math.pi / NLAT))
 
     sent = solve(source_coeffs, inverses, my_orders, rad_index)
-    early, sent = lax.optimization_barrier((fourier_orders, sent))
     coeffs = lax.all_to_all(sent, "rad", 0, 0, tiled=True)
     pairs = [lax.dynamic_slice_in_dim(v, rad_index * 2, 2, 0) for v in (my_orders[:16], my_orders[16:])]
     own_orders = jnp.concatenate(pairs * 2)
     (own,) = legendre_tables(own_orders, ((0, 8, 4, 0),), "legendre_own")
-    rows = phase_rows(early)
-    coeffs, own, rows = lax.optimization_barrier((coeffs, own, rows))
     fields = synth(coeffs, own, ints)
-    fields, late, rows = lax.optimization_barrier((fields, my_orders, rows))
+    fields, late, fourier_orders = lax.optimization_barrier((fields, my_orders, fourier_orders))
     fields = lax.all_to_all(fields, ("ang", "rad"), 0, 0, tiled=True)
     low, up = legendre_tables(late, ((0, 16, 16, 0), (16, 16, 16, 8)), "legendre")
-    tables = fourier_tables(rows, fourier_orders)
+    tables = fourier_tables(phase_rows(fourier_orders))
     fields, low, up, tables = lax.optimization_barrier((fields, low, up, tables))
     fourier = grid_stage(fields, velocity, tables, ints, sines)
     fourier = lax.all_to_all(fourier, "ang", 0, 0, tiled=True)

time: 155 us -> 140 us (0.903)
  Pallas kernels: 86.9 us -> 66.5 us
  waiting for transfers between devices: 3.73 us -> 16.8 us
  other arithmetic: 9.8 us -> 6.58 us
  starting transfers between devices: 16.3 us -> 13.8 us
    pallas_call x2, Pallas kernels: 38.7 us -> 24.6 us  [legendre_tables(): pl.pallas_call(functools.partial(legendre_kernel, groups), grid_spec=pltp...]
    all_to_all x1, waiting for transfers between devices: 3.72 us -> 13.7 us  [local(): fields = lax.all_to_all(fields, ('ang', 'rad'), 0, 0, tiled=True)]
    pallas_call x1, Pallas kernels: 11.9 us -> 7.24 us  [synth(): pl.pallas_call(synth_kernel, grid_spec=pltpu.PrefetchScalarGridSpec(num_s...]
    sin x2, other arithmetic: 6.95 us -> 3.58 us  [phase_rows(): return (jnp.cos(near), jnp.sin(near), jnp.cos(far), jnp.sin(far), weights)]
    all_to_all x1, waiting for transfers between devices: 0.01 us -> 3.09 us  [local(): coeffs = lax.all_to_all(sent, 'rad', 0, 0, tiled=True)]
    all_to_all x1, starting transfers between devices: 11.6 us -> 9.03 us  [local(): fields = lax.all_to_all(fields, ('ang', 'rad'), 0, 0, tiled=True)]
  transfers between devices with their start and end apart: 2 -> 2, of which waited for: 1 -> 2; matrix products, arithmetic and copies ran while one was open for 10% -> 8% of each run, Pallas kernels for 29% -> 21%
where the time goes in v3:
time: 140 us
  Pallas kernels  66.5 us (48%)
  blocking collectives  26.9 us (19%)
  waiting for transfers between devices  16.8 us (12%)
  starting transfers between devices  13.8 us (10%)
  local copies, waits for them, and re-layouts  8.87 us (6%)
  other arithmetic  6.58 us (5%)
    all_to_all x1, blocking collectives, local(): fourier = lax.all_to_all(fourier, 'ang', 0, 0, tiled=True)  26.9 us
    pallas_call x2, Pallas kernels, legendre_tables(): pl.pallas_call(functools.partial(legendre_kernel, groups), grid_spec=pltp...  24.6 us
    all_to_all x1, waiting for transfers between devices, local(): fields = lax.all_to_all(fields, ('ang', 'rad'), 0, 0, tiled=True)  13.7 us
    pallas_call x1, Pallas kernels, grid_stage(): pl.pallas_call(grid_kernel, grid_spec=pltpu.PrefetchScalarGridSpec(num_sc...  13.6 us
    pallas_call x1, Pallas kernels, analyse(): pl.pallas_call(analyse_body, grid_spec=pltpu.PrefetchScalarGridSpec(num_s...  10.7 us
    all_to_all x1, starting transfers between devices, local(): fields = lax.all_to_all(fields, ('ang', 'rad'), 0, 0, tiled=True)  9.03 us
    pallas_call x1, Pallas kernels, synth(): pl.pallas_call(synth_kernel, grid_spec=pltpu.PrefetchScalarGridSpec(num_s...  7.24 us
    pallas_call x1, Pallas kernels, solve(): pl.pallas_call(solve_kernel, grid_spec=pltpu.PrefetchScalarGridSpec(num_s...  5.47 us
  transfers between devices with their start and end apart: 2, of which 2 were waited for; matrix products, arithmetic and copies ran while one was open for 8% of the time, Pallas kernels for 21%

profile of v3, /device:TPU:0, one launch (start us, length us, event | category | flops | bytes accessed | tf_op | source)
XLA Modules:
  0.0 139.6 jit_solution(6148907290254463811)
XLA Ops:
  0.0 0.8 dynamic_slice.12
  0.8 0.1 broadcast_in_dim.54
  0.8 0.7 broadcast_in_dim.55.order_ref
  1.5 5.5 %solve.1 = bf16[8,512,128]{2,1,0:T(8,128)(2,1)} custom-call(s32[1]{0:T(128)} %bitcast.2.base_ref, bf16[32,128,128]{2,1,0:T(8,128)(2,1)} %bitcast.21, bf16[64,128,128]{2,1,0:T(8,128)(2,1)} %inv_ref.1, s32[64,128]{1,0:T(8,128)} %broadcast_in_dim.55.order_ref), custom_call_target="tpu_custom_call" | custom-call | flops 134217728 | bytes 4194304 | tf_op jit(solution)/shard_map/solve/pallas_call | solution.py:101
  7.0 4.7 %all-to-all-start = ((bf16[8,512,128]{2,1,0:T(8,128)(2,1)}), bf16[8,512,128]{2,1,0:T(8,128)(2,1)S(1)}, u32[]{:S(2)}, u32[]{:S(2)}) async-start(bf16[8,512,128]{2,1,0:T(8,128)(2,1)} %solve.1), calls=%async_computation | async-start | bytes 2097152 | tf_op jit(solution)/shard_map/all_to_all | solution.py:538
  12.2 0.6 gather_fusion
  12.9 0.1 reshape.298
  13.4 0.1 reshape.299
  13.6 0.1 reshape.300
  13.7 0.7 multiply_add_fusion.1.log_ref
  14.3 0.7 broadcast_in_dim.56.m_ref
  15.0 8.9 %legendre_own.1.leg_ref = bf16[4,512,384]{2,1,0:T(8,128)(2,1)} custom-call(f32[512]{0:T(512)} %constant.121.clone.c1_ref, f32[512]{0:T(512)} %constant.122.clone.c2_ref, f32[8,128]{1,0:T(8,128)} %broadcast_in_dim.56.m_ref, f32[16,384]{1,0:T(8,128)} %constant.118.clone.x_ref, f32[8,384]{1,0:T(8,128)} %multiply_add_fusion.1.log_ref), custom_call_target="tpu_custom_call" | custom-call | flops 16000000 | bytes 3200000 | tf_op jit(solution)/shard_map/legendre_own/pallas_call | solution.py:202
  23.9 0.7 pad_add_fusion.1.ints_ref
  24.6 3.1 %all-to-all-done.recv_ref = bf16[8,512,128]{2,1,0:T(8,128)(2,1)S(1)} async-done(((bf16[8,512,128]{2,1,0:T(8,128)(2,1)}), bf16[8,512,128]{2,1,0:T(8,128)(2,1)S(1)}, u32[]{:S(2)}, u32[]{:S(2)}) %all-to-all-start) | async-done | bytes 1048608 | tf_op jit(solution)/shard_map/all_to_all | solution.py:538
  27.7 1.0 copy-done.2
  28.6 7.2 %synth.1 = bf16[128,96,128]{2,1,0:T(8,128)(2,1)} custom-call(s32[4]{0:T(128)} %pad_add_fusion.1.ints_ref, bf16[8,512,128]{2,1,0:T(8,128)(2,1)} %copy-done.2, bf16[4,512,384]{2,1,0:T(8,128)(2,1)} %legendre_own.1.leg_ref, bf16[256,512]{1,0:T(8,128)(2,1)} %constant.124.mat_ref), custom_call_target="tpu_custom_call" | custom-call | flops 2000000000 | bytes 7000000 | tf_op jit(solution)/shard_map/synth/pallas_call | solution.py:327
  35.9 9.0 %all-to-all-start.1 = ((bf16[128,96,128]{2,1,0:T(8,128)(2,1)}), bf16[128,96,128]{2,1,0:T(8,128)(2,1)S(1)}, u32[]{:S(2)}, u32[]{:S(2)}) async-start(bf16[128,96,128]{2,1,0:T(8,128)(2,1)} %synth.1), calls=%async_computation.1 | async-start | bytes 6291456 | tf_op jit(solution)/shard_map/all_to_all | solution.py:544
  44.9 0.6 multiply_sine_fusion.1.sines_ref
  45.5 0.7 gather_fusion.1
  46.3 0.1 copy.47
  46.5 0.8 copy.48.w
  47.4 1.9 %fusion.4 = (f32[512,128]{1,0:T(8,128)}, f32[512,128]{1,0:T(8,128)}) fusion(s32[512]{0:T(512)S(1)} %pad_add_fusion), kind=kLoop, calls=%fused_computation.8 | loop fusion | flops 589824 | bytes 526336 | tf_op jit(solution)/shard_map/sin | solution.py:243
  49.3 1.6 %multiply_sine_fusion = (f32[512,8]{1,0:T(8,128)}, f32[512,8]{1,0:T(8,128)}) fusion(f32[512,8]{1,0:T(8,128)S(1)} %copy.47), kind=kLoop, calls=%fused_computation.11 | loop fusion | flops 4096 | bytes 49152 | tf_op jit(solution)/shard_map/sin | solution.py:243
  51.0 4.9 %tables.1 = (bf16[1024,768]{1,0:T(8,128)(2,1)}, bf16[1024,768]{1,0:T(8,128)(2,1)}, bf16[1024,768]{1,0:T(8,128)(2,1)}) custom-call(f32[512,128]{1,0:T(8,128)} %get-tuple-element.44.nc, f32[512,128]{1,0:T(8,128)} %get-tuple-element.43.ns, f32[512,8]{1,0:T(8,128)} %get-tuple-element.36.fc, f32[512,8]{1,0:T(8,128)} %get-tuple-element.35.fs, f32[512,8]{1,0:T(8,128)} %copy.48.w), custom_call_target="tpu_custom_call" | custom-call | flops 8000000 | bytes 8000000 | tf_op jit(solution)/shard_map/tables/pallas_call | solution.py:275
  55.8 0.7 multiply_add_fusion.log_ref
  56.5 0.7 broadcast_in_dim.57.m_ref
  57.2 15.7 %legendre.1 = (bf16[16,512,384]{2,1,0:T(8,128)(2,1)}, bf16[16,256,384]{2,1,0:T(8,128)(2,1)}) custom-call(f32[512]{0:T(512)} %constant.121.clone.c1_ref, f32[512]{0:T(512)} %constant.122.clone.c2_ref, f32[32,128]{1,0:T(8,128)} %broadcast_in_dim.57.m_ref, f32[16,384]{1,0:T(8,128)} %constant.118.clone.x_ref, f32[32,384]{1,0:T(8,128)} %multiply_add_fusion.log_ref), custom_call_target="tpu_custom_call" | custom-call | flops 64000000 | bytes 12800000 | tf_op jit(solution)/shard_map/legendre/pallas_call | solution.py:202
  72.9 13.7 %all-to-all-done.1 = bf16[128,96,128]{2,1,0:T(8,128)(2,1)S(1)} async-done(((bf16[128,96,128]{2,1,0:T(8,128)(2,1)}), bf16[128,96,128]{2,1,0:T(8,128)(2,1)S(1)}, u32[]{:S(2)}, u32[]{:S(2)}) %all-to-all-start.1) | async-done | bytes 3145760 | tf_op jit(solution)/shard_map/all_to_all | solution.py:544
  86.6 1.7 %copy-done.1 = bf16[128,96,128]{2,1,0:T(8,128)(2,1)} copy-done((bf16[128,96,128]{2,1,0:T(8,128)(2,1)}, bf16[128,96,128]{2,1,0:T(8,128)(2,1)S(1)}, u32[]{:S(2)}) %copy-start.1) | copy-done | bytes 3145752
  88.3 13.6 %grid.1 = bf16[16,48,1024]{2,1,0:T(8,128)(2,1)} custom-call(s32[4]{0:T(128)} %pad_add_fusion.1.ints_ref, f32[48]{0:T(128)} %multiply_sine_fusion.1.sines_ref, bf16[128,2,48,128]{3,2,1,0:T(8,128)(2,1)} %bitcast.20, bf16[2,48,16,1536]{3,2,1,0:T(8,128)(2,1)} %vel_ref.1, bf16[1024,768]{1,0:T(8,128)(2,1)} %get-tuple-element.28.t_ref, ...), custom_call_target="tpu_custom_call" | custom-call | flops 3700000000 | bytes 14000000 | tf_op jit(solution)/shard_map/grid/pallas_call | solution.py:416
  102.0 26.9 %all_to_all.15.recv_ref = bf16[16,48,1024]{2,1,0:T(8,128)(2,1)} all-to-all(bf16[16,48,1024]{2,1,0:T(8,128)(2,1)} %grid.1), channel_id=1, replica_groups=mesh['rad'=8,'ang'=16] {'ang'}, dimensions={0} | all-to-all | bytes 3145728 | tf_op jit(solution)/shard_map/all_to_all | solution.py:549
  128.9 10.7 %analyse.1 = bf16[2,16,2,16,512]{4,3,2,1,0:T(8,128)(2,1)} custom-call(s32[16]{0:T(128)} %copy-done.4, bf16[16,48,1024]{2,1,0:T(8,128)(2,1)} %all_to_all.15.recv_ref, bf16[16,512,384]{2,1,0:T(8,128)(2,1)} %get-tuple-element.31.low_ref, bf16[16,256,384]{2,1,0:T(8,128)(2,1)} %get-tuple-element.32.up_ref), custom_call_target="tpu_custom_call" | custom-call | flops 1200000000 | bytes 12000000 | tf_op jit(solution)/shard_map/analyse/pallas_call | solution.py:491
  (35 shorter events, 1.1 us)
Async XLA Ops:
  7.0 5.2 %copy-start = (f32[512]{0:T(512)S(1)}, f32[512]{0:T(512)}, u32[]{:S(2)}) copy-start(f32[512]{0:T(512)} %constant.119.clone) | copy-start | bytes 6148
  7.0 5.9 %copy-start.5 = (s32[512]{0:T(512)S(1)}, s32[512]{0:T(512)}, u32[]{:S(2)}) copy-start(s32[512]{0:T(512)} %param.18) | copy-start | bytes 6148
  7.0 6.7 %copy-start.3 = (f32[384]{0:T(512)S(1)}, f32[384]{0:T(512)}, u32[]{:S(2)}) copy-start(f32[384]{0:T(512)} %constant.120.clone) | copy-start | bytes 4612
  7.0 20.7 %all-to-all-start = ((bf16[8,512,128]{2,1,0:T(8,128)(2,1)}), bf16[8,512,128]{2,1,0:T(8,128)(2,1)S(1)}, u32[]{:S(2)}, u32[]{:S(2)}) async-start(bf16[8,512,128]{2,1,0:T(8,128)(2,1)} %solve.1), calls=%async_computation | async-start | bytes 2097152 | tf_op jit(solution)/shard_map/all_to_all | solution.py:538
  11.8 24.1 %copy-start.4 = (s32[16]{0:T(128)}, s32[16]{0:T(128)S(1)}, u32[]{:S(2)}) copy-start(s32[16]{0:T(128)S(1)} %get-tuple-element.48.par_ref) | copy-start | bytes 196
  27.7 1.0 copy-start.2
  35.9 50.7 %all-to-all-start.1 = ((bf16[128,96,128]{2,1,0:T(8,128)(2,1)}), bf16[128,96,128]{2,1,0:T(8,128)(2,1)S(1)}, u32[]{:S(2)}, u32[]{:S(2)}) async-start(bf16[128,96,128]{2,1,0:T(8,128)(2,1)} %synth.1), calls=%async_computation.1 | async-start | bytes 6291456 | tf_op jit(solution)/shard_map/all_to_all | solution.py:544
  86.6 1.7 %copy-start.1 = (bf16[128,96,128]{2,1,0:T(8,128)(2,1)}, bf16[128,96,128]{2,1,0:T(8,128)(2,1)S(1)}, u32[]{:S(2)}) copy-start(bf16[128,96,128]{2,1,0:T(8,128)(2,1)S(1)} %all-to-all-done.1) | copy-start | bytes 9437188

commit v4 on v3

--- a/solution.py
+++ b/solution.py
@@ -40,6 +40,10 @@
 
 def params(sem=("arbitrary",)):
     return pltpu.CompilerParams(dimension_semantics=sem, vmem_limit_bytes=vmem_bytes)
+
+
+def in_vmem(x):
+    return pltpu.with_memory_space_constraint(x, pltpu.VMEM)
 
 
 def swap_chunks(x0, x1, x2, x3):
@@ -57,7 +61,7 @@
     return (y0, y1, y2, y3)
 
 
-def solve_kernel(base_ref, src_ref, inv_ref, order_ref, out_ref, wide, acc):
+def solve_kernel(src_ref, inv_ref, out_ref, wide, acc):
     step = pl.program_id(0)
     steps = pl.num_programs(0)
     block = inv_ref.shape[0]
@@ -69,8 +73,6 @@
             return 0
 
         lax.fori_loop(0, 32, widen, 0, unroll=4)
-
-    order = order_ref[...]
 
     def degree(i, _):
         row = step * block + i
@@ -78,7 +80,6 @@
         x1 = wide[pl.ds(2 * row + 1, 32, stride=136), :]
         x = jnp.concatenate([x0, x1], 0).astype(bf16)
         y = lax.dot_general(x, inv_ref[i], NT, preferred_element_type=f32)
-        y = jnp.where(order <= base_ref[0] + row, y, 0.0)
         acc[pl.ds(row, 64, stride=72), :] = y
         return 0
 
@@ -95,27 +96,21 @@
                         out_ref[r, row : row + 64, :] = acc[plane * 72 : plane * 72 + 64, :].astype(bf16)
 
 
-def solve(source, inverses, orders, rad_index):
-    src = source.reshape(32, 128, 128)
-    order = jnp.broadcast_to(jnp.tile(orders, 2)[:, None], (64, 128))
+def solve(source, inverses):
     return pl.pallas_call(
         solve_kernel,
-        grid_spec=pltpu.PrefetchScalarGridSpec(
-            num_scalar_prefetch=1,
-            grid=(4,),
-            in_specs=[
-                pl.BlockSpec((32, 128, 128), lambda g, b: (0, 0, 0)),
-                pl.BlockSpec((16, 128, 128), lambda g, b: (g, 0, 0)),
-                pl.BlockSpec((64, 128), lambda g, b: (0, 0)),
-            ],
-            out_specs=pl.BlockSpec((8, 512, 128), lambda g, b: (0, 0, 0)),
-            scratch_shapes=[pltpu.VMEM((32 * 136, 128), f32), pltpu.VMEM((64 * 72, 128), f32)],
-        ),
+        grid=(4,),
+        in_specs=[
+            pl.BlockSpec((32, 128, 128), lambda g: (0, 0, 0)),
+            pl.BlockSpec((16, 128, 128), lambda g: (g, 0, 0)),
+        ],
+        out_specs=pl.BlockSpec((8, 512, 128), lambda g: (0, 0, 0)),
         out_shape=jax.ShapeDtypeStruct((8, 512, 128), bf16),
+        scratch_shapes=[pltpu.VMEM((32 * 136, 128), f32), pltpu.VMEM((64 * 72, 128), f32)],
         compiler_params=params(),
         cost_estimate=pl.CostEstimate(flops=134217728, bytes_accessed=4194304, transcendentals=0),
         name="solve",
-    )(jnp.reshape(rad_index * 64, (1,)), src, inverses, order)
+    )(source.reshape(32, 128, 128), inverses)
 
 
 def legendre_kernel(groups, c1_ref, c2_ref, m_ref, x_ref, log_ref, *refs):
@@ -298,7 +293,8 @@
                 planes.append(recv_ref[first:8, row : row + 64, :].reshape(count, 128))
             coeffs = jnp.concatenate(planes, 1)
             rad = jnp.dot(coeffs, mat, preferred_element_type=f32)
-            degree = lax.broadcasted_iota(jnp.int32, rad.shape, 0)
+            degree = lax.broadcasted_iota(jnp.int32, rad.shape, 0) + 64 * first
+            rad = jnp.where(degree >= ints_ref[4 + 2 * lu + q], rad, 0.0)
             sign = (1 - 2 * ((degree + h) % 2)).astype(f32)
             both = jnp.concatenate([rad.astype(bf16), (rad * sign).astype(bf16)], 1)
             table = leg_ref[lu * 2 + q, 64 * first : LMAX, :]
@@ -330,7 +326,7 @@
             num_scalar_prefetch=1,
             grid=(1,),
             in_specs=[
-                pl.BlockSpec((8, 512, 128), lambda g, b: (0, 0, 0)),
+                pl.BlockSpec(memory_space=pltpu.VMEM),
                 pl.BlockSpec((4, LMAX, HALF), lambda g, b: (0, 0, 0)),
                 pl.BlockSpec((256, 512), lambda g, b: (0, 0)),
             ],
@@ -341,7 +337,7 @@
         compiler_params=params(),
         cost_estimate=pl.CostEstimate(flops=2000000000, bytes_accessed=7000000, transcendentals=0),
         name="synth",
-    )(ints, recv, table, radial_matrix())
+    )(ints, in_vmem(recv), table, radial_matrix())
 
 
 def grid_kernel(
@@ -349,11 +345,12 @@
     wide, l0e, l0o, l1e, l1o, se, so, ze, zo, ue, uo, oe, oo,
 ):
     step = pl.program_id(0)
+    now = pl.ds(pl.multiple_of(step * 16, 16), 16)
 
     def widen(u, _):
         row = pl.multiple_of(u * 40, 8)
-        wide[pl.ds(row, 16), :] = recv_ref[u, 0].astype(f32)
-        wide[pl.ds(row + 16, 16), :] = recv_ref[u, 1].astype(f32)
+        wide[pl.ds(row, 16), :] = recv_ref[u, 0, now, :].astype(f32)
+        wide[pl.ds(row + 16, 16), :] = recv_ref[u, 1, now, :].astype(f32)
         return 0
 
     lax.fori_loop(0, 128, widen, 0, unroll=8)
@@ -419,7 +416,7 @@
             num_scalar_prefetch=2,
             grid=(3,),
             in_specs=[
-                pl.BlockSpec((128, 2, 16, 128), lambda g, *_: (0, 0, g, 0)),
+                pl.BlockSpec(memory_space=pltpu.VMEM),
                 pl.BlockSpec((2, 16, 16, NLON), latitude_block),
                 whole,
                 whole,
@@ -436,7 +433,7 @@
         compiler_params=params(),
         cost_estimate=pl.CostEstimate(flops=3700000000, bytes_accessed=14000000, transcendentals=0),
         name="grid",
-    )(ints, sines, recv.reshape(128, 2, 48, 128), velocity, *tables)
+    )(ints, sines, in_vmem(recv.reshape(128, 2, 48, 128)), velocity, *tables)
 
 
 def analyse_body(par_ref, recv_ref, low_ref, up_ref, out_ref, plus, minus, part_p, part_m):
@@ -454,16 +451,16 @@
             for b in range(3):
                 rows = slice(128 * b, 128 * b + 128)
                 for part, dst in ((part_p, plus), (part_m, minus)):
-                    turned = part[rows, :].T
+                    turned = part[rows, :].astype(bf16).T.astype(f32)
                     dst[b, 144 * t : 144 * t + 64, :] = turned[0:64]
                     dst[b, 144 * t + 72 : 144 * t + 136, :] = turned[64:128]
 
-    for q in range(2):
-        pair = step * 2 + q
+    for q in range(4):
+        pair = step * 4 + q
         h0 = par_ref[pair]
         for lu in range(2):
             h = h0 if lu == 0 else 1 - h0
-            base = h * 32 + q * 16 + step
+            base = h * 32 + (q % 2) * 16 + step * 2 + q // 2
             left = jnp.concatenate(
                 [
                     jnp.concatenate([ref[b, pl.ds(base + 8 * c, 16, stride=72), :] for b in range(3)], 1)
@@ -487,16 +484,16 @@
 
 
 def analyse(recv, low, up, parity):
-    out = pl.BlockSpec((2, 2, 2, 16, LMAX), lambda g, *_: (0, g, 0, 0, 0))
+    out = pl.BlockSpec((2, 4, 2, 16, LMAX), lambda g, *_: (0, g, 0, 0, 0))
     return pl.pallas_call(
         analyse_body,
         grid_spec=pltpu.PrefetchScalarGridSpec(
             num_scalar_prefetch=1,
-            grid=(8,),
+            grid=(4,),
             in_specs=[
                 pl.BlockSpec((16, 48, 1024), lambda g, *_: (0, 0, 0), pipeline_mode=pl.Buffered(1)),
-                pl.BlockSpec((2, LMAX, HALF), lambda g, *_: (g, 0, 0)),
-                pl.BlockSpec((2, LMAX // 2, HALF), lambda g, *_: (g, 0, 0)),
+                pl.BlockSpec((4, LMAX, HALF), lambda g, *_: (g, 0, 0)),
+                pl.BlockSpec((4, LMAX // 2, HALF), lambda g, *_: (g, 0, 0)),
             ],
             out_specs=out,
             scratch_shapes=[
@@ -526,18 +523,18 @@
     fourier_orders = jnp.concatenate(by_parity)
     my_orders = lax.dynamic_slice_in_dim(order_slots, ang_index * 32, 32, 0)
     parity = my_orders[:16] % 2
+    pairs = [lax.dynamic_slice_in_dim(v, rad_index * 2, 2, 0) for v in (my_orders[:16], my_orders[16:])]
+    own_orders = jnp.concatenate(pairs * 2)
     south = (ang_index >= 8).astype(jnp.int32)
     ints = jnp.concatenate(
-        [rad_index[None].astype(jnp.int32), lax.dynamic_slice_in_dim(parity, rad_index * 2, 2, 0), south[None]]
+        [rad_index[None].astype(jnp.int32), lax.dynamic_slice_in_dim(parity, rad_index * 2, 2, 0), south[None], own_orders[:4]]
     )
     position = jnp.arange(48, dtype=jnp.int32)
     latitude = ang_index * 48 + jnp.where(south == 1, 47 - position, position)
     sines = jnp.sin((latitude.astype(f32) + 0.5) * (math.pi / NLAT))
 
-    sent = solve(source_coeffs, inverses, my_orders, rad_index)
+    sent = solve(source_coeffs, inverses)
     coeffs = lax.all_to_all(sent, "rad", 0, 0, tiled=True)
-    pairs = [lax.dynamic_slice_in_dim(v, rad_index * 2, 2, 0) for v in (my_orders[:16], my_orders[16:])]
-    own_orders = jnp.concatenate(pairs * 2)
     (own,) = legendre_tables(own_orders, ((0, 8, 4, 0),), "legendre_own")
     fields = synth(coeffs, own, ints)
     fields, late, fourier_orders = lax.optimization_barrier((fields, my_orders, fourier_orders))

time: 140 us -> 133 us (0.950)
  local copies, waits for them, and re-layouts: 8.87 us -> 5.41 us
  Pallas kernels: 66.5 us -> 63.7 us
    unnamed x12 -> x8, local copies, waits for them, and re-layouts: 2.69 us -> 0.01 us
    pallas_call x1, Pallas kernels: 10.7 us -> 8.48 us  [analyse(): pl.pallas_call(analyse_body, grid_spec=pltpu.PrefetchScalarGridSpec(num_s...]
  transfers between devices with their start and end apart: 2 -> 2, of which waited for: 2 -> 2; matrix products, arithmetic and copies ran while one was open for 8% -> 9% of each run, Pallas kernels for 21% -> 22%
where the time goes in v4:
time: 133 us
  Pallas kernels  63.7 us (48%)
  blocking collectives  26.9 us (20%)
  waiting for transfers between devices  16.8 us (13%)
  starting transfers between devices  13.8 us (10%)
  other arithmetic  5.92 us (4%)
  local copies, waits for them, and re-layouts  5.41 us (4%)
    all_to_all x1, blocking collectives, local(): fourier = lax.all_to_all(fourier, 'ang', 0, 0, tiled=True)  26.9 us
    pallas_call x2, Pallas kernels, legendre_tables(): pl.pallas_call(functools.partial(legendre_kernel, groups), grid_spec=pltp...  24.6 us
    all_to_all x1, waiting for transfers between devices, local(): fields = lax.all_to_all(fields, ('ang', 'rad'), 0, 0, tiled=True)  13.7 us
    pallas_call x1, Pallas kernels, grid_stage(): pl.pallas_call(grid_kernel, grid_spec=pltpu.PrefetchScalarGridSpec(num_sc...  13.4 us
    all_to_all x1, starting transfers between devices, local(): fields = lax.all_to_all(fields, ('ang', 'rad'), 0, 0, tiled=True)  9.04 us
    pallas_call x1, Pallas kernels, analyse(): pl.pallas_call(analyse_body, grid_spec=pltpu.PrefetchScalarGridSpec(num_s...  8.48 us
    pallas_call x1, Pallas kernels, synth(): pl.pallas_call(synth_kernel, grid_spec=pltpu.PrefetchScalarGridSpec(num_s...  6.98 us
    pallas_call x1, Pallas kernels, solve(): pl.pallas_call(solve_kernel, grid=(4,), in_specs=[pl.BlockSpec((32, 128,...  5.45 us
  transfers between devices with their start and end apart: 2, of which 2 were waited for; matrix products, arithmetic and copies ran while one was open for 9% of the time, Pallas kernels for 22%

profile of v4, /device:TPU:0, one launch (start us, length us, event | category | flops | bytes accessed | tf_op | source)
XLA Modules:
  0.0 132.6 jit_solution(6894165758203530567)
XLA Ops:
  0.0 5.4 %solve.1 = bf16[8,512,128]{2,1,0:T(8,128)(2,1)} custom-call(bf16[32,128,128]{2,1,0:T(8,128)(2,1)} %bitcast.20, bf16[64,128,128]{2,1,0:T(8,128)(2,1)} %inv_ref.1), custom_call_target="tpu_custom_call" | custom-call | flops 134217728 | bytes 4194304 | tf_op jit(solution)/shard_map/solve/pallas_call | solution.py:100
  5.5 4.7 %all-to-all-start = ((bf16[8,512,128]{2,1,0:T(8,128)(2,1)}), bf16[8,512,128]{2,1,0:T(8,128)(2,1)S(1)}, u32[]{:S(2)}, u32[]{:S(2)}) async-start(bf16[8,512,128]{2,1,0:T(8,128)(2,1)} %solve.1), calls=%async_computation | async-start | bytes 2097152 | tf_op jit(solution)/shard_map/all_to_all | solution.py:537
  10.6 0.1 reshape.292
  10.7 0.1 dynamic_slice.13
  10.9 0.6 gather_fusion
  11.6 0.1 and_select_fusion.2
  11.8 0.1 copy.45
  11.9 0.1 reshape.293
  12.0 0.1 copy.46
  12.1 0.1 reshape.294
  12.2 0.7 concatenate.49.ints_ref
  12.8 0.7 multiply_add_fusion.1.log_ref
  13.5 0.7 broadcast_in_dim.26.m_ref
  14.2 8.9 %legendre_own.1.leg_ref = bf16[4,512,384]{2,1,0:T(8,128)(2,1)} custom-call(f32[512]{0:T(512)} %constant.119.clone.c1_ref, f32[512]{0:T(512)} %constant.120.clone.c2_ref, f32[8,128]{1,0:T(8,128)} %broadcast_in_dim.26.m_ref, f32[16,384]{1,0:T(8,128)} %constant.116.clone.x_ref, f32[8,384]{1,0:T(8,128)} %multiply_add_fusion.1.log_ref), custom_call_target="tpu_custom_call" | custom-call | flops 16000000 | bytes 3200000 | tf_op jit(solution)/shard_map/legendre_own/pallas_call | solution.py:197
  23.1 3.0 %all-to-all-done.recv_ref = bf16[8,512,128]{2,1,0:T(8,128)(2,1)S(1)} async-done(((bf16[8,512,128]{2,1,0:T(8,128)(2,1)}), bf16[8,512,128]{2,1,0:T(8,128)(2,1)S(1)}, u32[]{:S(2)}, u32[]{:S(2)}) %all-to-all-start) | async-done | bytes 1048608 | tf_op jit(solution)/shard_map/all_to_all | solution.py:537
  26.1 7.0 %synth.1 = bf16[128,96,128]{2,1,0:T(8,128)(2,1)} custom-call(s32[8]{0:T(128)} %concatenate.49.ints_ref, bf16[8,512,128]{2,1,0:T(8,128)(2,1)S(1)} %all-to-all-done.recv_ref, bf16[4,512,384]{2,1,0:T(8,128)(2,1)} %legendre_own.1.leg_ref, bf16[256,512]{1,0:T(8,128)(2,1)} %constant.122.mat_ref), custom_call_target="tpu_custom_call" | custom-call | flops 2000000000 | bytes 7000000 | tf_op jit(solution)/shard_map/synth/pallas_call | solution.py:323
  33.1 9.0 %all-to-all-start.1 = ((bf16[128,96,128]{2,1,0:T(8,128)(2,1)}), bf16[128,96,128]{2,1,0:T(8,128)(2,1)S(1)}, u32[]{:S(2)}, u32[]{:S(2)}) async-start(bf16[128,96,128]{2,1,0:T(8,128)(2,1)} %synth.1), calls=%async_computation.1 | async-start | bytes 6291456 | tf_op jit(solution)/shard_map/all_to_all | solution.py:541
  42.2 0.6 multiply_sine_fusion.1.sines_ref
  42.8 0.7 gather_fusion.1
  43.5 0.1 fusion.7
  43.6 0.1 copy.47
  43.7 0.9 copy.48.w
  44.6 1.9 %fusion.4 = (f32[512,128]{1,0:T(8,128)}, f32[512,128]{1,0:T(8,128)}) fusion(s32[512]{0:T(512)S(1)} %pad_add_fusion), kind=kLoop, calls=%fused_computation.8 | loop fusion | flops 589824 | bytes 526336 | tf_op jit(solution)/shard_map/sin | solution.py:238
  46.6 1.6 %multiply_sine_fusion = (f32[512,8]{1,0:T(8,128)}, f32[512,8]{1,0:T(8,128)}) fusion(f32[512,8]{1,0:T(8,128)S(1)} %copy.47), kind=kLoop, calls=%fused_computation.11 | loop fusion | flops 4096 | bytes 49152 | tf_op jit(solution)/shard_map/sin | solution.py:238
  48.2 4.9 %tables.1 = (bf16[1024,768]{1,0:T(8,128)(2,1)}, bf16[1024,768]{1,0:T(8,128)(2,1)}, bf16[1024,768]{1,0:T(8,128)(2,1)}) custom-call(f32[512,128]{1,0:T(8,128)} %get-tuple-element.44.nc, f32[512,128]{1,0:T(8,128)} %get-tuple-element.43.ns, f32[512,8]{1,0:T(8,128)} %get-tuple-element.36.fc, f32[512,8]{1,0:T(8,128)} %get-tuple-element.35.fs, f32[512,8]{1,0:T(8,128)} %copy.48.w), custom_call_target="tpu_custom_call" | custom-call | flops 8000000 | bytes 8000000 | tf_op jit(solution)/shard_map/tables/pallas_call | solution.py:270
  53.1 0.7 multiply_add_fusion.log_ref
  53.8 0.7 broadcast_in_dim.48.m_ref
  54.4 15.7 %legendre.1 = (bf16[16,512,384]{2,1,0:T(8,128)(2,1)}, bf16[16,256,384]{2,1,0:T(8,128)(2,1)}) custom-call(f32[512]{0:T(512)} %constant.119.clone.c1_ref, f32[512]{0:T(512)} %constant.120.clone.c2_ref, f32[32,128]{1,0:T(8,128)} %broadcast_in_dim.48.m_ref, f32[16,384]{1,0:T(8,128)} %constant.116.clone.x_ref, f32[32,384]{1,0:T(8,128)} %multiply_add_fusion.log_ref), custom_call_target="tpu_custom_call" | custom-call | flops 64000000 | bytes 12800000 | tf_op jit(solution)/shard_map/legendre/pallas_call | solution.py:197
  70.1 13.7 %all-to-all-done.1 = bf16[128,96,128]{2,1,0:T(8,128)(2,1)S(1)} async-done(((bf16[128,96,128]{2,1,0:T(8,128)(2,1)}), bf16[128,96,128]{2,1,0:T(8,128)(2,1)S(1)}, u32[]{:S(2)}, u32[]{:S(2)}) %all-to-all-start.1) | async-done | bytes 3145760 | tf_op jit(solution)/shard_map/all_to_all | solution.py:541
  83.8 13.4 %grid.1 = bf16[16,48,1024]{2,1,0:T(8,128)(2,1)} custom-call(s32[8]{0:T(128)} %concatenate.49.ints_ref, f32[48]{0:T(128)} %multiply_sine_fusion.1.sines_ref, bf16[128,2,48,128]{3,2,1,0:T(8,128)(2,1)S(1)} %bitcast.19, bf16[2,48,16,1536]{3,2,1,0:T(8,128)(2,1)} %vel_ref.1, bf16[1024,768]{1,0:T(8,128)(2,1)} %get-tuple-element.28.t_ref, ...), custom_call_target="tpu_custom_call" | custom-call | flops 3700000000 | bytes 14000000 | tf_op jit(solution)/shard_map/grid/pallas_call | solution.py:413
  97.2 26.9 %all_to_all.15.recv_ref = bf16[16,48,1024]{2,1,0:T(8,128)(2,1)} all-to-all(bf16[16,48,1024]{2,1,0:T(8,128)(2,1)} %grid.1), channel_id=1, replica_groups=mesh['rad'=8,'ang'=16] {'ang'}, dimensions={0} | all-to-all | bytes 3145728 | tf_op jit(solution)/shard_map/all_to_all | solution.py:546
  124.2 8.5 %analyse.1 = bf16[2,16,2,16,512]{4,3,2,1,0:T(8,128)(2,1)} custom-call(s32[16]{0:T(128)} %copy-done.2, bf16[16,48,1024]{2,1,0:T(8,128)(2,1)} %all_to_all.15.recv_ref, bf16[16,512,384]{2,1,0:T(8,128)(2,1)} %get-tuple-element.31.low_ref, bf16[16,256,384]{2,1,0:T(8,128)(2,1)} %get-tuple-element.32.up_ref), custom_call_target="tpu_custom_call" | custom-call | flops 1200000000 | bytes 12000000 | tf_op jit(solution)/shard_map/analyse/pallas_call | solution.py:488
  (28 shorter events, 0.8 us)
Async XLA Ops:
  5.4 4.7 %copy-start.3 = (s32[512]{0:T(512)S(1)}, s32[512]{0:T(512)}, u32[]{:S(2)}) copy-start(s32[512]{0:T(512)} %param.18) | copy-start | bytes 6148
  5.5 5.5 %copy-start = (f32[512]{0:T(512)S(1)}, f32[512]{0:T(512)}, u32[]{:S(2)}) copy-start(f32[512]{0:T(512)} %constant.117.clone) | copy-start | bytes 6148
  5.5 7.4 %copy-start.1 = (f32[384]{0:T(512)S(1)}, f32[384]{0:T(512)}, u32[]{:S(2)}) copy-start(f32[384]{0:T(512)} %constant.118.clone) | copy-start | bytes 4612
  5.5 20.7 %all-to-all-start = ((bf16[8,512,128]{2,1,0:T(8,128)(2,1)}), bf16[8,512,128]{2,1,0:T(8,128)(2,1)S(1)}, u32[]{:S(2)}, u32[]{:S(2)}) async-start(bf16[8,512,128]{2,1,0:T(8,128)(2,1)} %solve.1), calls=%async_computation | async-start | bytes 2097152 | tf_op jit(solution)/shard_map/all_to_all | solution.py:537
  10.3 22.8 %copy-start.2 = (s32[16]{0:T(128)}, s32[16]{0:T(128)S(1)}, u32[]{:S(2)}) copy-start(s32[16]{0:T(128)S(1)} %get-tuple-element.48.par_ref) | copy-start | bytes 196
  33.1 50.7 %all-to-all-start.1 = ((bf16[128,96,128]{2,1,0:T(8,128)(2,1)}), bf16[128,96,128]{2,1,0:T(8,128)(2,1)S(1)}, u32[]{:S(2)}, u32[]{:S(2)}) async-start(bf16[128,96,128]{2,1,0:T(8,128)(2,1)} %synth.1), calls=%async_computation.1 | async-start | bytes 6291456 | tf_op jit(solution)/shard_map/all_to_all | solution.py:541
